TPU v7x, 32 devices: a whole 2x2x4 slice. The times are simulated.
32 devices in a mesh: dp: 8 (over z, y), tensor: 4 (over x, core).
Axes of the slice: x: 2, y: 2, z: 4, core: 2. Of those that a mesh axis runs over, the one named last changes fastest.
Arguments:
- tokens: bfloat16 [8192, 768], P(('dp', 'tensor')), may hold values from -6 to 6
- qkv_weight: bfloat16 [2, 768, 3, 768], P(None, None, None, 'tensor'), may hold values from -0.21875 to 0.21875
- qv_bias: bfloat16 [2, 2, 768], P(None, None, 'tensor'), may hold values from -3 to 3
- out_weight: bfloat16 [2, 768, 768], P(None, 'tensor'), may hold values from -0.625 to 0.625
- up_weight: bfloat16 [2, 768, 3072], P(None, None, 'tensor'), may hold values from -0.21875 to 0.21875
- up_bias: bfloat16 [2, 3072], P(None, 'tensor'), may hold values from -3 to 3
- down_weight: bfloat16 [2, 3072, 768], P(None, 'tensor'), may hold values from -0.109375 to 0.109375
- out_bias: bfloat16 [2, 4, 768], replicated, may hold values from -2.5 to 2.5
- norm_gain: bfloat16 [2, 2, 768], replicated, may hold values from 0.25 to 1.75
- doc_start: int32 [32], P('dp'), may hold values from 0 to 3, as said below
- picture: int32 [32], P('dp'), may hold values 0 or 1
- cotangent: bfloat16 [8192, 768], P(('dp', 'tensor')), may hold values from -6 to 6
Outputs:
- result: float32 [8192, 768], P(('dp', 'tensor'))
- tokens_grad: float32 [8192, 768], P(('dp', 'tensor'))
- qkv_weight_grad: float32 [2, 768, 3, 768], P(None, 'dp', None, 'tensor')
- qv_bias_grad: float32 [2, 2, 768], P(None, None, ('tensor', 'dp'))
- out_weight_grad: float32 [2, 768, 768], P(None, 'tensor', 'dp')
- up_weight_grad: float32 [2, 768, 3072], P(None, 'dp', 'tensor')
- up_bias_grad: float32 [2, 3072], P(None, ('tensor', 'dp'))
- down_weight_grad: float32 [2, 3072, 768], P(None, 'tensor', 'dp')
- out_bias_grad: float32 [2, 4, 768], P(None, None, ('dp', 'tensor'))
- norm_gain_grad: float32 [2, 2, 768], P(None, None, ('dp', 'tensor'))
Inputs may be any that keep to these rules, and one draw needn't show every extreme that they name: `doc_start`: A block's 1024 tokens (one index of dp) are whole documents made of whole 256-token spans; entry b is the first span of span b's document counted from the start of its block, so it never exceeds b and stays constant inside a document; every block holds one document of exactly 768 tokens and none longer.
All inputs are finite; a program needn't handle non-finite values. No bound on the sum of `picture` on one device may be relied on, other than what follows from the above.
Results may differ from a plain program's by a relative error of at most 0.03.
Values may be sent and summed in bfloat16 or wider, within the bound.
A program may use at most 192 MiB of HBM per device.

v0:
```python
from functools import partial

import jax
import jax.numpy as jnp
from jax import lax
from jax.sharding import PartitionSpec as P

HEAD_DIM = 64
SPAN = 256


epsilon = 1e-05


def layer_norm(inputs, gain, shift):
    average = jnp.mean(inputs, axis=-1, keepdims=True)
    centered = inputs - average
    variance = jnp.mean(centered * centered, axis=-1, keepdims=True)
    return centered * lax.rsqrt(variance + epsilon) * gain + shift


def block_mask(doc_tokens, picture_tokens, begin_row, end_row):
    query_pos = jnp.arange(begin_row, end_row)
    key_pos = jnp.arange(end_row)
    same_doc = doc_tokens[begin_row:end_row, None] == doc_tokens[None, :end_row]
    earlier = key_pos[None, :] <= query_pos[:, None]
    same_span = query_pos[:, None] // SPAN == key_pos[None, :] // SPAN
    picture_row = picture_tokens[begin_row:end_row, None] == 1
    return same_doc & (earlier | same_span & picture_row)


def block_scores(query_rows, key_rows, doc_tokens, picture_tokens, begin_row, end_row):
    heads_here = query_rows.shape[1] // HEAD_DIM
    query_block = query_rows[begin_row:end_row].reshape(end_row - begin_row, heads_here, HEAD_DIM)
    key_part = key_rows[:end_row].reshape(end_row, heads_here, HEAD_DIM)
    scores = (
        jnp.einsum("qhd,khd->hqk", query_block, key_part, preferred_element_type=jnp.float32)
        * 0.125
    )
    allowed = block_mask(doc_tokens, picture_tokens, begin_row, end_row)
    return (jnp.where(allowed[None], scores, -1e30), query_block, key_part)


def attention_forward(query_rows, key_rows, value_rows, doc_tokens, picture_tokens, block_rows):
    seq_rows, local_width = query_rows.shape
    heads_here = local_width // HEAD_DIM
    outputs = []
    log_totals = []
    for begin_row in range(0, seq_rows, block_rows):
        end_row = begin_row + block_rows
        scores, query_block, key_part = block_scores(
            query_rows, key_rows, doc_tokens, picture_tokens, begin_row, end_row
        )
        row_max = jnp.max(scores, axis=-1, keepdims=True)
        exponent = jnp.exp(scores - row_max)
        row_total = jnp.sum(exponent, axis=-1, keepdims=True)
        probability = (exponent / row_total).astype(jnp.bfloat16)
        value_part = value_rows[:end_row].reshape(end_row, heads_here, HEAD_DIM)
        attended = jnp.einsum(
            "hqk,khd->qhd", probability, value_part, preferred_element_type=jnp.float32
        )
        outputs.append(attended.reshape(block_rows, local_width).astype(jnp.bfloat16))
        log_totals.append(row_max + jnp.log(row_total))
    return (jnp.concatenate(outputs, axis=0), log_totals)


def attention_backward(
    query_rows,
    key_rows,
    value_rows,
    grad_attended,
    log_totals,
    doc_tokens,
    picture_tokens,
    block_rows,
):
    seq_rows, local_width = query_rows.shape
    heads_here = local_width // HEAD_DIM
    grad_query_blocks = []
    grad_keys = jnp.zeros((seq_rows, heads_here, HEAD_DIM), jnp.float32)
    grad_values = jnp.zeros((seq_rows, heads_here, HEAD_DIM), jnp.float32)
    for block_idx, begin_row in enumerate(range(0, seq_rows, block_rows)):
        end_row = begin_row + block_rows
        scores, query_block, key_part = block_scores(
            query_rows, key_rows, doc_tokens, picture_tokens, begin_row, end_row
        )
        probability = jnp.exp(scores - log_totals[block_idx])
        prob_low = probability.astype(jnp.bfloat16)
        value_part = value_rows[:end_row].reshape(end_row, heads_here, HEAD_DIM)
        grad_block = grad_attended[begin_row:end_row].reshape(block_rows, heads_here, HEAD_DIM)
        grad_prob = jnp.einsum(
            "qhd,khd->hqk", grad_block, value_part, preferred_element_type=jnp.float32
        )
        row_inner = jnp.sum(probability * grad_prob, axis=-1, keepdims=True)
        grad_scores = (probability * (grad_prob - row_inner)).astype(jnp.bfloat16)
        grad_query = (
            jnp.einsum("hqk,khd->qhd", grad_scores, key_part, preferred_element_type=jnp.float32)
            * 0.125
        )
        grad_query_blocks.append(grad_query.reshape(block_rows, local_width).astype(jnp.bfloat16))
        grad_keys = grad_keys.at[:end_row].add(
            jnp.einsum("hqk,qhd->khd", grad_scores, query_block, preferred_element_type=jnp.float32)
            * 0.125
        )
        grad_values = grad_values.at[:end_row].add(
            jnp.einsum("hqk,qhd->khd", prob_low, grad_block, preferred_element_type=jnp.float32)
        )
    grad_query_all = jnp.concatenate(grad_query_blocks, axis=0)
    return (
        grad_query_all,
        grad_keys.reshape(seq_rows, local_width).astype(jnp.bfloat16),
        grad_values.reshape(seq_rows, local_width).astype(jnp.bfloat16),
    )


def body(
    tokens,
    qkv_weight,
    qv_bias,
    out_weight,
    up_weight,
    up_bias,
    down_weight,
    out_bias,
    norm_gain,
    doc_start,
    picture,
    cotangent,
):
    layers = qkv_weight.shape[0]
    rows_here = tokens.shape[0]
    doc_tokens = jnp.repeat(doc_start, SPAN)
    picture_tokens = jnp.repeat(picture, SPAN)
    seq_rows = doc_tokens.shape[0]
    block_rows = min(512, seq_rows)
    exact_gelu = partial(jax.nn.gelu, approximate=False)
    stream = tokens.astype(jnp.float32)
    stored = []
    for layer_idx in range(layers):
        rows_in = lax.all_gather(stream.astype(jnp.bfloat16), "tensor", axis=0, tiled=True)
        projected = jnp.einsum(
            "td,dcf->tcf", rows_in, qkv_weight[layer_idx], preferred_element_type=jnp.float32
        )
        query_rows = (projected[:, 0] + qv_bias[layer_idx, 0]).astype(jnp.bfloat16)
        key_rows = projected[:, 1].astype(jnp.bfloat16)
        value_rows = (projected[:, 2] + qv_bias[layer_idx, 1]).astype(jnp.bfloat16)
        attended, log_totals = attention_forward(
            query_rows, key_rows, value_rows, doc_tokens, picture_tokens, block_rows
        )
        attn_weight = out_weight[layer_idx]

        def attn_rows(begin_row, row_count, source=attended, weight_rows=attn_weight):
            return jnp.dot(
                lax.dynamic_slice_in_dim(source, begin_row, row_count, 0),
                weight_rows,
                preferred_element_type=jnp.float32,
            )

        branch = lax.psum_scatter(
            attn_rows(jnp.int32(0), rows_here * lax.axis_size("tensor")).astype(jnp.bfloat16),
            "tensor",
            scatter_dimension=0,
            tiled=True,
        ).astype(jnp.float32)
        normed, first_pull = jax.vjp(
            layer_norm,
            stream + branch + out_bias[layer_idx, 0].astype(jnp.float32),
            norm_gain[layer_idx, 0].astype(jnp.float32),
            out_bias[layer_idx, 1].astype(jnp.float32),
        )
        normed_rows = lax.all_gather(normed.astype(jnp.bfloat16), "tensor", axis=0, tiled=True)
        pre_act = (
            jnp.dot(normed_rows, up_weight[layer_idx], preferred_element_type=jnp.float32)
            + up_bias[layer_idx]
        )
        activation_f, gelu_pull = jax.vjp(exact_gelu, pre_act)
        activation = activation_f.astype(jnp.bfloat16)
        ffn_weight = down_weight[layer_idx]

        def ffn_rows(begin_row, row_count, source=activation, weight_rows=ffn_weight):
            return jnp.dot(
                lax.dynamic_slice_in_dim(source, begin_row, row_count, 0),
                weight_rows,
                preferred_element_type=jnp.float32,
            )

        branch_two = lax.psum_scatter(
            ffn_rows(jnp.int32(0), rows_here * lax.axis_size("tensor")).astype(jnp.bfloat16),
            "tensor",
            scatter_dimension=0,
            tiled=True,
        ).astype(jnp.float32)
        stream, second_pull = jax.vjp(
            layer_norm,
            normed + branch_two + out_bias[layer_idx, 2].astype(jnp.float32),
            norm_gain[layer_idx, 1].astype(jnp.float32),
            out_bias[layer_idx, 3].astype(jnp.float32),
        )
        stored.append(
            (
                rows_in,
                query_rows,
                key_rows,
                value_rows,
                attended,
                log_totals,
                first_pull,
                normed_rows,
                gelu_pull,
                activation,
                second_pull,
            )
        )
    grad_stream = cotangent.astype(jnp.float32)
    local_terms = [None] * layers
    vector_terms = [None] * layers
    for layer_idx in reversed(range(layers)):
        (
            rows_in,
            query_rows,
            key_rows,
            value_rows,
            attended,
            log_totals,
            first_pull,
            normed_rows,
            gelu_pull,
            activation,
            second_pull,
        ) = stored[layer_idx]
        grad_second, grad_gain_two, grad_shift_two = second_pull(grad_stream)
        grad_ffn_bias = jnp.sum(grad_second, axis=0)
        ffn_grad_rows = lax.all_gather(
            grad_second.astype(jnp.bfloat16), "tensor", axis=0, tiled=True
        )
        down_grad = jnp.einsum(
            "tf,td->fd", activation, ffn_grad_rows, preferred_element_type=jnp.float32
        )
        grad_activation = jnp.einsum(
            "td,fd->tf", ffn_grad_rows, down_weight[layer_idx], preferred_element_type=jnp.float32
        )
        grad_pre = gelu_pull(grad_activation)[0].astype(jnp.bfloat16)
        up_bias_grad = jnp.sum(grad_pre, axis=0, dtype=jnp.float32)
        up_grad = jnp.einsum("td,tf->df", normed_rows, grad_pre, preferred_element_type=jnp.float32)
        up_rows = up_weight[layer_idx]

        def ffn_back_rows(begin_row, row_count, source=grad_pre, weight_rows=up_rows):
            return jnp.einsum(
                "tf,df->td",
                lax.dynamic_slice_in_dim(source, begin_row, row_count, 0),
                weight_rows,
                preferred_element_type=jnp.float32,
            )

        grad_normed = grad_second + lax.psum_scatter(
            ffn_back_rows(jnp.int32(0), rows_here * lax.axis_size("tensor")).astype(jnp.bfloat16),
            "tensor",
            scatter_dimension=0,
            tiled=True,
        ).astype(jnp.float32)
        grad_first, grad_gain_one, grad_shift_one = first_pull(grad_normed)
        grad_attn_bias = jnp.sum(grad_first, axis=0)
        attn_grad_rows = lax.all_gather(
            grad_first.astype(jnp.bfloat16), "tensor", axis=0, tiled=True
        )
        out_grad = jnp.einsum(
            "tf,td->fd", attended, attn_grad_rows, preferred_element_type=jnp.float32
        )
        grad_attended = jnp.einsum(
            "td,fd->tf", attn_grad_rows, out_weight[layer_idx], preferred_element_type=jnp.float32
        ).astype(jnp.bfloat16)
        grad_query, grad_keys, grad_values = attention_backward(
            query_rows,
            key_rows,
            value_rows,
            grad_attended,
            log_totals,
            doc_tokens,
            picture_tokens,
            block_rows,
        )
        grad_stack = jnp.stack((grad_query, grad_keys, grad_values), axis=1)
        qkv_grad = jnp.einsum(
            "td,tcf->dcf", rows_in, grad_stack, preferred_element_type=jnp.float32
        )
        head_bias_grad = jnp.stack(
            (
                jnp.sum(grad_query, axis=0, dtype=jnp.float32),
                jnp.sum(grad_values, axis=0, dtype=jnp.float32),
            )
        )
        proj_rows = qkv_weight[layer_idx]

        def attn_back_rows(begin_row, row_count, source=grad_stack, weight_rows=proj_rows):
            return jnp.einsum(
                "tcf,dcf->td",
                lax.dynamic_slice_in_dim(source, begin_row, row_count, 0),
                weight_rows,
                preferred_element_type=jnp.float32,
            )

        grad_stream = grad_first + lax.psum_scatter(
            attn_back_rows(jnp.int32(0), rows_here * lax.axis_size("tensor")).astype(jnp.bfloat16),
            "tensor",
            scatter_dimension=0,
            tiled=True,
        ).astype(jnp.float32)
        layer_terms = (qkv_grad, head_bias_grad, out_grad, up_grad, up_bias_grad, down_grad)
        vector_terms[layer_idx] = (
            jnp.stack((grad_attn_bias, grad_shift_one, grad_ffn_bias, grad_shift_two)),
            jnp.stack((grad_gain_one, grad_gain_two)),
        )
        local_terms[layer_idx] = layer_terms
    stacked = tuple(
        (
            jnp.stack([local_terms[layer_idx][member] for layer_idx in range(layers)])
            for member in range(6)
        )
    )
    summed = (
        lax.psum_scatter(stacked[0], "dp", scatter_dimension=1, tiled=True),
        lax.psum_scatter(stacked[1], "dp", scatter_dimension=2, tiled=True),
        lax.psum_scatter(stacked[2], "dp", scatter_dimension=2, tiled=True),
        lax.psum_scatter(stacked[3], "dp", scatter_dimension=1, tiled=True),
        lax.psum_scatter(stacked[4], "dp", scatter_dimension=1, tiled=True),
        lax.psum_scatter(stacked[5], "dp", scatter_dimension=2, tiled=True),
    )
    bias_rows = jnp.stack([vector_terms[layer_idx][0] for layer_idx in range(layers)])
    gain_rows = jnp.stack([vector_terms[layer_idx][1] for layer_idx in range(layers)])
    bias_part, gain_part = (
        lax.psum_scatter(bias_rows, ("dp", "tensor"), scatter_dimension=2, tiled=True),
        lax.psum_scatter(gain_rows, ("dp", "tensor"), scatter_dimension=2, tiled=True),
    )
    return (
        stream,
        grad_stream,
        summed[0],
        summed[1],
        summed[2],
        summed[3],
        summed[4],
        summed[5],
        bias_part,
        gain_part,
    )


def solution(mesh):
    return jax.shard_map(
        body,
        mesh=mesh,
        in_specs=(
            P(("dp", "tensor"), None),
            P(None, None, None, "tensor"),
            P(None, None, "tensor"),
            P(None, "tensor", None),
            P(None, None, "tensor"),
            P(None, "tensor"),
            P(None, "tensor", None),
            P(),
            P(),
            P("dp"),
            P("dp"),
            P(("dp", "tensor"), None),
        ),
        out_specs=(
            P(("dp", "tensor"), None),
            P(("dp", "tensor"), None),
            P(None, "dp", None, "tensor"),
            P(None, None, ("tensor", "dp")),
            P(None, "tensor", "dp"),
            P(None, "dp", "tensor"),
            P(None, ("tensor", "dp")),
            P(None, "tensor", "dp"),
            P(None, None, ("dp", "tensor")),
            P(None, None, ("dp", "tensor")),
        ),
        check_vma=False,
    )
```

profile of v0, /device:TPU:0, one launch (start us, length us, event | category | flops | bytes accessed | tf_op | source)
XLA Modules:
  0.0 1025.4 jit_solution(8624559352223935676)
XLA Ops:
  15.4 16.6 %all-gather.9.cloned.1.call-done = bf16[1024,768]{1,0:T(8,128)(2,1)} async-done(((bf16[256,768]{1,0:T(8,128)(2,1)}), bf16[1024,768]{1,0:T(8,128)(2,1)}) %all-gather.9.cloned.1.call-update) | async-done | bytes 1572880 | tf_op jit(solution)/shard_map/all_gather | solution.py:140
  46.3 27.5 %reduce-scatter.22.cloned.1.call-done = bf16[256,768]{1,0:T(8,128)(2,1)} async-done(((bf16[1024,768]{1,0:T(8,128)(2,1)}), bf16[256,768]{1,0:T(8,128)(2,1)}) %reduce-scatter.22.cloned.1.call-update) | async-done | bytes 393232 | tf_op jit(solution)/shard_map/reduce_scatter | solution.py:159
  79.6 18.6 %all-gather.11.cloned.1.call-done = bf16[1024,768]{1,0:T(8,128)(2,1)} async-done(((bf16[256,768]{1,0:T(8,128)(2,1)}), bf16[1024,768]{1,0:T(8,128)(2,1)}) %all-gather.11.cloned.1.call-update) | async-done | bytes 1572880 | tf_op jit(solution)/shard_map/all_gather | solution.py:171
  98.2 11.7 %multiply_convert_fusion.5 = (bf16[1024,768]{1,0:T(8,128)(2,1)S(1)}, f32[1024,768]{1,0:T(8,128)}, f32[1024,768]{1,0:T(8,128)}) fusion(f32[768]{0:T(1024)S(1)} %get-tuple-element.186, bf16[1024,768]{1,0:T(8,128)(2,1)} %all-gather.11.cloned.1.call-done, bf16[2,768,768]{2,1,0:T(8,128)(2,1)} %param.40), kind=kOutput, calls=%fused_computation.55 | convolution fusion | flops 1259864064 | bytes 10619904 | tf_op jit(solution)/shard_map/dot_general | solution.py:173
  113.7 28.3 %reduce-scatter.24.cloned.1.call-done = bf16[256,768]{1,0:T(8,128)(2,1)} async-done(((bf16[1024,768]{1,0:T(8,128)(2,1)}), bf16[256,768]{1,0:T(8,128)(2,1)}) %reduce-scatter.24.cloned.1.call-update) | async-done | bytes 393232 | tf_op jit(solution)/shard_map/reduce_scatter | solution.py:187
  146.1 18.9 %all-gather.13.cloned.1.call-done = bf16[1024,768]{1,0:T(8,128)(2,1)} async-done(((bf16[256,768]{1,0:T(8,128)(2,1)}), bf16[1024,768]{1,0:T(8,128)(2,1)}) %all-gather.13.cloned.1.call-update) | async-done | bytes 1572880 | tf_op jit(solution)/shard_map/all_gather | solution.py:140
  179.0 28.3 %reduce-scatter.26.cloned.1.call-done = bf16[256,768]{1,0:T(8,128)(2,1)} async-done(((bf16[1024,768]{1,0:T(8,128)(2,1)}), bf16[256,768]{1,0:T(8,128)(2,1)}) %reduce-scatter.26.cloned.1.call-update) | async-done | bytes 393232 | tf_op jit(solution)/shard_map/reduce_scatter | solution.py:159
  212.3 19.6 %all-gather.15.cloned.1.call-done = bf16[1024,768]{1,0:T(8,128)(2,1)} async-done(((bf16[256,768]{1,0:T(8,128)(2,1)}), bf16[1024,768]{1,0:T(8,128)(2,1)}) %all-gather.15.cloned.1.call-update) | async-done | bytes 1572880 | tf_op jit(solution)/shard_map/all_gather | solution.py:171
  231.8 11.7 %multiply_convert_fusion.4 = (bf16[1024,768]{1,0:T(8,128)(2,1)S(1)}, f32[1024,768]{1,0:T(8,128)}, f32[1024,768]{1,0:T(8,128)}) fusion(f32[768]{0:T(1024)} %get-tuple-element.185, bf16[1024,768]{1,0:T(8,128)(2,1)} %all-gather.15.cloned.1.call-done, bf16[2,768,768]{2,1,0:T(8,128)(2,1)} %param.40), kind=kOutput, calls=%fused_computation.39 | convolution fusion | flops 1259864064 | bytes 10620928 | tf_op jit(solution)/shard_map/dot_general | solution.py:173
  247.3 28.3 %reduce-scatter.28.cloned.1.call-done = bf16[256,768]{1,0:T(8,128)(2,1)} async-done(((bf16[1024,768]{1,0:T(8,128)(2,1)}), bf16[256,768]{1,0:T(8,128)(2,1)}) %reduce-scatter.28.cloned.1.call-update) | async-done | bytes 393232 | tf_op jit(solution)/shard_map/reduce_scatter | solution.py:187
  282.6 19.8 %all-gather.17.cloned.1.call-done = bf16[1024,768]{1,0:T(8,128)(2,1)} async-done(((bf16[256,768]{1,0:T(8,128)(2,1)}), bf16[1024,768]{1,0:T(8,128)(2,1)}) %all-gather.17.cloned.1.call-update) | async-done | bytes 1572880 | tf_op jit(solution)/shard_map/all_gather | solution.py:233
  302.3 6.6 convert_reduce_fusion
  312.8 28.3 %reduce-scatter.30.cloned.1.call-done = bf16[256,768]{1,0:T(8,128)(2,1)} async-done(((bf16[1024,768]{1,0:T(8,128)(2,1)}), bf16[256,768]{1,0:T(8,128)(2,1)}) %reduce-scatter.30.cloned.1.call-update) | async-done | bytes 393232 | tf_op jit(solution)/shard_map/reduce_scatter | solution.py:255
  350.5 17.3 %all-gather.19.cloned.1.call-done = bf16[1024,768]{1,0:T(8,128)(2,1)} async-done(((bf16[256,768]{1,0:T(8,128)(2,1)}), bf16[1024,768]{1,0:T(8,128)(2,1)}) %all-gather.19.cloned.1.call-update) | async-done | bytes 1572880 | tf_op jit(solution)/shard_map/all_gather | solution.py:263
  385.5 28.3 %reduce-scatter.32.cloned.1.call-done = bf16[256,768]{1,0:T(8,128)(2,1)} async-done(((bf16[1024,768]{1,0:T(8,128)(2,1)}), bf16[256,768]{1,0:T(8,128)(2,1)}) %reduce-scatter.32.cloned.1.call-update) | async-done | bytes 393232 | tf_op jit(solution)/shard_map/reduce_scatter | solution.py:302
  418.5 19.6 %all-gather.21.cloned.1.call-done = bf16[1024,768]{1,0:T(8,128)(2,1)} async-done(((bf16[256,768]{1,0:T(8,128)(2,1)}), bf16[1024,768]{1,0:T(8,128)(2,1)}) %all-gather.21.cloned.1.call-update) | async-done | bytes 1572880 | tf_op jit(solution)/shard_map/all_gather | solution.py:233
  438.1 6.0 convert_reduce_fusion.1
  447.9 28.3 %reduce-scatter.34.cloned.1.call-done = bf16[256,768]{1,0:T(8,128)(2,1)} async-done(((bf16[1024,768]{1,0:T(8,128)(2,1)}), bf16[256,768]{1,0:T(8,128)(2,1)}) %reduce-scatter.34.cloned.1.call-update) | async-done | bytes 393232 | tf_op jit(solution)/shard_map/reduce_scatter | solution.py:255
  481.5 4.8 convolution_bitcast_fusion
  487.4 3.6 convolution_bitcast_fusion.1
  493.5 8.2 copy.40
  508.8 3.4 reshape.1117
  534.8 4.7 copy.51
  539.6 8.0 reshape.1113
  558.9 7.4 reduce-scatter.44.cloned.1.call-done
  567.8 43.4 %all-reduce.8 = (f32[2,4,768]{2,1,0:T(4,128)S(1)}, f32[2,2,768]{2,1,0:T(2,128)S(1)}) all-reduce(f32[2,4,768]{2,1,0:T(4,128)S(1)} %pad_maximum_fusion.16, f32[2,2,768]{2,1,0:T(2,128)S(1)} %pad_maximum_fusion.17), channel_id=16, replica_groups=mesh['dp'=8,'tensor'=4] {'dp','tensor'}, use_global_device_ids=true, to_apply=%region_56.57.clone | all-reduce | flops 9216 | bytes 73728
  612.6 127.3 %all-reduce.11.cloned.1.call-done = f32[2,768,768]{1,0,2:T(2,128)} async-done(((f32[2,768,768]{1,0,2:T(2,128)}), f32[2,768,768]{1,0,2:T(2,128)}) %all-reduce.11.cloned.1.call-update) | async-done | bytes 4718608
  742.1 19.4 %all-reduce.4 = f32[2,2,192]{2,1,0:T(2,128)S(1)} all-reduce(f32[2,2,192]{2,1,0:T(2,128)S(1)} %pad_maximum_fusion.19), channel_id=11, replica_groups=mesh['dp'=8,'tensor'=4] {'dp'}, use_global_device_ids=true, to_apply=%region_41.42.clone | all-reduce | flops 768 | bytes 6144
  762.1 44.4 %reduce-scatter.42.cloned.1.call-done = f32[96,384]{1,0:T(8,128)} async-done(((f32[768,384]{1,0:T(8,128)}), f32[96,384]{1,0:T(8,128)}) %reduce-scatter.42.cloned.1.call-update) | async-done | bytes 147472
  808.4 28.0 %reduce-scatter.36.cloned.1.call-done = bf16[256,768]{1,0:T(8,128)(2,1)} async-done(((bf16[1024,768]{1,0:T(8,128)(2,1)}), bf16[256,768]{1,0:T(8,128)(2,1)}) %reduce-scatter.36.cloned.1.call-update) | async-done | bytes 393232 | tf_op jit(solution)/shard_map/reduce_scatter | solution.py:302
  838.4 80.6 %reduce-scatter.40.cloned.1.call-done = f32[96,1152]{1,0:T(8,128)} async-done(((f32[768,1152]{1,0:T(8,128)}), f32[96,1152]{1,0:T(8,128)}) %reduce-scatter.40.cloned.1.call-update) | async-done | bytes 442384
  921.6 96.5 %reduce-scatter.38.cloned.1.call-done = f32[2,96,768]{2,1,0:T(8,128)} async-done(((f32[2,768,768]{2,1,0:T(8,128)}), f32[2,96,768]{2,1,0:T(8,128)}) %reduce-scatter.38.cloned.1.call-update) | async-done | bytes 589840 | tf_op jit(solution)/shard_map/reduce_scatter | solution.py:324
  (526 shorter events, 164.1 us)
Async XLA Ops:
  7.2 24.8 %all-gather.9.cloned.1.call-start = ((), (), s32[]{:S(2)}) async-start(), calls=%async_computation.12 | async-start | bytes 1966080 | tf_op jit(solution)/shard_map/all_gather | solution.py:140
  7.9 66.0 %reduce-scatter.22.cloned.1.call-start = ((), (), s32[]{:S(2)}) async-start(), calls=%async_computation.13 | async-start | bytes 1966080 | tf_op jit(solution)/shard_map/reduce_scatter | solution.py:159
  43.8 35.2 %copy-start.116 = (bf16[2,768]{1,0:T(2,128)(2,1)S(1)}, bf16[2,768]{1,0:T(2,128)(2,1)}, u32[]{:S(2)}) copy-start(bf16[2,768]{1,0:T(2,128)(2,1)} %param.41) | copy-start | bytes 9220
  45.6 52.6 %all-gather.11.cloned.1.call-start = ((), (), s32[]{:S(2)}) async-start(), calls=%async_computation.14 | async-start | bytes 1966080 | tf_op jit(solution)/shard_map/all_gather | solution.py:171
  46.3 97.4 %copy-start.87 = (f32[768]{0:T(1024)}, f32[768]{0:T(1024)S(1)}, u32[]{:S(2)}) copy-start(f32[768]{0:T(1024)S(1)} %get-tuple-element.176) | copy-start | bytes 9220
  46.3 160.9 %copy-start.73 = (f32[768]{0:T(1024)}, f32[768]{0:T(1024)S(1)}, u32[]{:S(2)}) copy-start(f32[768]{0:T(1024)S(1)} %get-tuple-element.266) | copy-start | bytes 9220
  75.1 66.9 %copy-start.82 = (f32[256]{0:T(256)}, f32[256]{0:T(256)S(1)}, u32[]{:S(2)}) copy-start(f32[256]{0:T(256)S(1)} %broadcast_multiply_fusion.3) | copy-start | bytes 3076
  76.4 65.6 %copy-start.94 = (f32[256]{0:T(256)}, f32[256]{0:T(256)S(1)}, u32[]{:S(2)}) copy-start(f32[256]{0:T(256)S(1)} %fusion.147) | copy-start | bytes 3076
  78.4 63.6 %reduce-scatter.24.cloned.1.call-start = ((), (), s32[]{:S(2)}) async-start(), calls=%async_computation.15 | async-start | bytes 1966080 | tf_op jit(solution)/shard_map/reduce_scatter | solution.py:187
  113.6 51.4 %all-gather.13.cloned.1.call-start = ((), (), s32[]{:S(2)}) async-start(), calls=%async_computation.16 | async-start | bytes 1966080 | tf_op jit(solution)/shard_map/all_gather | solution.py:140
  145.3 62.0 %reduce-scatter.26.cloned.1.call-start = ((), (), s32[]{:S(2)}) async-start(), calls=%async_computation.17 | async-start | bytes 1966080 | tf_op jit(solution)/shard_map/reduce_scatter | solution.py:159
  178.9 52.9 %all-gather.15.cloned.1.call-start = ((), (), s32[]{:S(2)}) async-start(), calls=%async_computation.18 | async-start | bytes 1966080 | tf_op jit(solution)/shard_map/all_gather | solution.py:171
  212.0 63.6 %reduce-scatter.28.cloned.1.call-start = ((), (), s32[]{:S(2)}) async-start(), calls=%async_computation.19 | async-start | bytes 1966080 | tf_op jit(solution)/shard_map/reduce_scatter | solution.py:187
  247.3 55.0 %all-gather.17.cloned.1.call-start = ((), (), s32[]{:S(2)}) async-start(), calls=%async_computation.20 | async-start | bytes 1966080 | tf_op jit(solution)/shard_map/all_gather | solution.py:233
  282.5 58.6 %reduce-scatter.30.cloned.1.call-start = ((), (), s32[]{:S(2)}) async-start(), calls=%async_computation.21 | async-start | bytes 1966080 | tf_op jit(solution)/shard_map/reduce_scatter | solution.py:255
  312.8 55.1 %all-gather.19.cloned.1.call-start = ((), (), s32[]{:S(2)}) async-start(), calls=%async_computation.22 | async-start | bytes 1966080 | tf_op jit(solution)/shard_map/all_gather | solution.py:263
  348.0 65.8 %reduce-scatter.32.cloned.1.call-start = ((), (), s32[]{:S(2)}) async-start(), calls=%async_computation.23 | async-start | bytes 1966080 | tf_op jit(solution)/shard_map/reduce_scatter | solution.py:302
  385.5 52.6 %copy-start.130 = (f32[768]{0:T(1024)S(1)}, f32[768]{0:T(1024)}, u32[]{:S(2)}) copy-start(f32[768]{0:T(1024)} %copy-done.129) | copy-start | bytes 9220
  385.5 52.6 %all-gather.21.cloned.1.call-start = ((), (), s32[]{:S(2)}) async-start(), calls=%async_computation.24 | async-start | bytes 1966080 | tf_op jit(solution)/shard_map/all_gather | solution.py:233
  418.3 57.9 %reduce-scatter.34.cloned.1.call-start = ((), (), s32[]{:S(2)}) async-start(), calls=%async_computation.25 | async-start | bytes 1966080 | tf_op jit(solution)/shard_map/reduce_scatter | solution.py:255
  447.8 33.7 %copy-start.131 = (f32[768]{0:T(1024)S(1)}, f32[768]{0:T(1024)}, u32[]{:S(2)}) copy-start(f32[768]{0:T(1024)} %get-tuple-element.256) | copy-start | bytes 9220
  447.8 56.9 %all-gather.23.cloned.1.call-start = ((), (), s32[]{:S(2)}) async-start(), calls=%async_computation.26 | async-start | bytes 1966080 | tf_op jit(solution)/shard_map/all_gather | solution.py:263
  481.4 84.8 %reduce-scatter.44.cloned.1.call-start = ((), (), s32[]{:S(2)}) async-start(), calls=%async_computation.31 | async-start | bytes 442368
  487.3 252.5 %all-reduce.11.cloned.1.call-start = ((), (), s32[]{:S(2)}) async-start(), calls=%async_computation.32 | async-start | bytes 9437184
  501.7 304.8 %reduce-scatter.42.cloned.1.call-start = ((), (), s32[]{:S(2)}) async-start(), calls=%async_computation.30 | async-start | bytes 1327104
  515.1 321.3 %reduce-scatter.36.cloned.1.call-start = ((), (), s32[]{:S(2)}) async-start(), calls=%async_computation.27 | async-start | bytes 1966080 | tf_op jit(solution)/shard_map/reduce_scatter | solution.py:302
  530.6 388.4 %reduce-scatter.40.cloned.1.call-start = ((), (), s32[]{:S(2)}) async-start(), calls=%async_computation.29 | async-start | bytes 3981312
  547.6 470.5 %reduce-scatter.38.cloned.1.call-start = ((), (), s32[]{:S(2)}) async-start(), calls=%async_computation.28 | async-start | bytes 5308416 | tf_op jit(solution)/shard_map/reduce_scatter | solution.py:324
  556.0 185.9 %copy-start.36 = (bf16[3,64,512]{2,1,0:T(8,128)(2,1)S(1)}, bf16[3,64,512]{2,1,0:T(8,128)(2,1)}, u32[]{:S(2)}) copy-start(bf16[3,64,512]{2,1,0:T(8,128)(2,1)} %copy-done.35) | copy-start | bytes 589828
  556.0 185.9 %copy-start.46 = (bf16[3,64,512]{2,1,0:T(8,128)(2,1)S(1)}, bf16[3,64,512]{2,1,0:T(8,128)(2,1)}, u32[]{:S(2)}) copy-start(bf16[3,64,512]{2,1,0:T(8,128)(2,1)} %copy-done.45) | copy-start | bytes 589828
  556.1 280.4 %copy-start.14 = (f32[256,768]{1,0:T(8,128)S(1)}, f32[256,768]{1,0:T(8,128)}, u32[]{:S(2)}) copy-start(f32[256,768]{1,0:T(8,128)} %copy-done.13) | copy-start | bytes 2359300
  556.1 280.3 %copy-start.118 = (f32[256]{0:T(256)S(1)}, f32[256]{0:T(256)}, u32[]{:S(2)}) copy-start(f32[256]{0:T(256)} %copy-done.117) | copy-start | bytes 3076
  (140 other events, 957.6 us)
Sparse Core Ops, SparseCore 0:
  9.6 22.3 all-gather.8
  45.7 28.1 reduce-scatter.21
  78.5 19.6 all-gather.10
  113.7 28.1 reduce-scatter.23
  145.4 19.6 all-gather.12
  179.1 28.1 reduce-scatter.25
  212.1 19.6 all-gather.14
  247.4 28.1 reduce-scatter.27
  282.6 19.6 all-gather.16
  312.9 28.1 reduce-scatter.29
  348.1 19.6 all-gather.18
  385.6 28.1 reduce-scatter.31
  418.4 19.6 all-gather.20
  447.9 28.1 reduce-scatter.33
  481.6 19.6 all-gather.22
  504.7 61.4 reduce-scatter.43
  570.1 169.6 all-reduce.10
  743.5 63.0 reduce-scatter.41
  809.2 27.1 reduce-scatter.35
  839.9 79.1 reduce-scatter.39
  923.2 94.7 reduce-scatter.37
where the time goes:
time: 1030 us
  waiting for transfers between devices  713 us (69%)
  matrix products  110 us (11%)
  local copies, waits for them, and re-layouts  63.2 us (6%)
  blocking collectives  62.8 us (6%)
  other arithmetic  55.9 us (5%)
  between operations  18.2 us (2%)
    unnamed x25, waiting for transfers between devices  261 us
    reduce_scatter x1, waiting for transfers between devices, body(): lax.psum_scatter(stacked[3], 'dp', scatter_dimension=1, tiled=True)  96.5 us
    unnamed x2, blocking collectives  62.8 us
    reduce_scatter x2, waiting for transfers between devices, body(): lax.psum_scatter(ffn_rows(jnp.int32(0), rows_here * lax.axis_size('tensor...  56.6 us
    reduce_scatter x2, waiting for transfers between devices, body(): lax.psum_scatter(ffn_back_rows(jnp.int32(0), rows_here * lax.axis_size('t...  56.5 us
    reduce_scatter x2, waiting for transfers between devices, body(): lax.psum_scatter(attn_back_rows(jnp.int32(0), rows_here * lax.axis_size('...  56.2 us
    reduce_scatter x2, waiting for transfers between devices, body(): lax.psum_scatter(attn_rows(jnp.int32(0), rows_here * lax.axis_size('tenso...  55.8 us
    unnamed x323, local copies, waits for them, and re-layouts  50.1 us
  transfers between devices with their start and end apart: 21, of which 20 were waited for; matrix products, arithmetic and copies ran while one was open for 9% of the time, Pallas kernels for 0%

commit v1 on v0

--- a/solution.py
+++ b/solution.py
@@ -311,37 +311,69 @@
             jnp.stack((grad_gain_one, grad_gain_two)),
         )
         local_terms[layer_idx] = layer_terms
-    stacked = tuple(
-        (
-            jnp.stack([local_terms[layer_idx][member] for layer_idx in range(layers)])
-            for member in range(6)
-        )
-    )
-    summed = (
-        lax.psum_scatter(stacked[0], "dp", scatter_dimension=1, tiled=True),
-        lax.psum_scatter(stacked[1], "dp", scatter_dimension=2, tiled=True),
-        lax.psum_scatter(stacked[2], "dp", scatter_dimension=2, tiled=True),
-        lax.psum_scatter(stacked[3], "dp", scatter_dimension=1, tiled=True),
-        lax.psum_scatter(stacked[4], "dp", scatter_dimension=1, tiled=True),
-        lax.psum_scatter(stacked[5], "dp", scatter_dimension=2, tiled=True),
-    )
-    bias_rows = jnp.stack([vector_terms[layer_idx][0] for layer_idx in range(layers)])
-    gain_rows = jnp.stack([vector_terms[layer_idx][1] for layer_idx in range(layers)])
-    bias_part, gain_part = (
-        lax.psum_scatter(bias_rows, ("dp", "tensor"), scatter_dimension=2, tiled=True),
-        lax.psum_scatter(gain_rows, ("dp", "tensor"), scatter_dimension=2, tiled=True),
+    shares = lax.axis_size("dp")
+    split = lax.axis_size("tensor")
+    width = tokens.shape[1]
+    rows_each = width // shares
+    head_each = qv_bias.shape[2] // shares
+    up_each = up_bias.shape[1] // shares
+    packed = []
+    for layer_idx in range(layers):
+        qkv_grad, head_bias_grad, out_grad, up_grad, up_bias_grad, down_grad = local_terms[layer_idx]
+        local_width = qkv_grad.shape[2]
+        hidden = up_grad.shape[1]
+        total_width = 4 * local_width + 2 * hidden
+        vectors = jnp.concatenate(vector_terms[layer_idx], axis=0)
+        extra = jnp.concatenate(
+            (
+                vectors.reshape(6, shares, rows_each).transpose(1, 0, 2).reshape(shares, -1),
+                head_bias_grad.reshape(2, shares, head_each).transpose(1, 0, 2).reshape(shares, -1),
+                up_bias_grad.reshape(shares, up_each),
+            ),
+            axis=1,
+        )
+        extra = jnp.pad(extra, ((0, 0), (0, -extra.shape[1] % total_width)))
+        extra = extra.reshape(shares, -1, total_width)
+        whole = jnp.concatenate(
+            (qkv_grad.reshape(width, -1), out_grad.T, up_grad, down_grad.T), axis=1
+        ).reshape(shares, rows_each, total_width)
+        whole = jnp.concatenate((whole, extra), axis=1).astype(jnp.bfloat16)
+        packed.append(
+            lax.psum_scatter(whole, "dp", scatter_dimension=0, tiled=True)[0].astype(jnp.float32)
+        )
+    qkv_parts, head_parts, out_parts, up_parts, up_bias_parts, down_parts, vector_parts = (
+        [],
+        [],
+        [],
+        [],
+        [],
+        [],
+        [],
+    )
+    for part in packed:
+        main, extra = part[:rows_each], part[rows_each:].reshape(-1)
+        vector_parts.append(extra[: 6 * rows_each].reshape(6, rows_each))
+        extra = extra[6 * rows_each :]
+        head_parts.append(extra[: 2 * head_each].reshape(2, head_each))
+        up_bias_parts.append(extra[2 * head_each : 2 * head_each + up_each])
+        qkv_parts.append(main[:, : 3 * local_width].reshape(rows_each, 3, local_width))
+        out_parts.append(main[:, 3 * local_width : 4 * local_width].T)
+        up_parts.append(main[:, 4 * local_width : 4 * local_width + hidden])
+        down_parts.append(main[:, 4 * local_width + hidden :].T)
+    vector_sum = lax.psum_scatter(
+        jnp.stack(vector_parts), "tensor", scatter_dimension=2, tiled=True
     )
     return (
         stream,
         grad_stream,
-        summed[0],
-        summed[1],
-        summed[2],
-        summed[3],
-        summed[4],
-        summed[5],
-        bias_part,
-        gain_part,
+        jnp.stack(qkv_parts),
+        jnp.stack(head_parts),
+        jnp.stack(out_parts),
+        jnp.stack(up_parts),
+        jnp.stack(up_bias_parts),
+        jnp.stack(down_parts),
+        vector_sum[:, :4],
+        vector_sum[:, 4:],
     )
 
 

time: 1030 us -> 765 us (0.74)
  waiting for transfers between devices: 713 us -> 469 us
  blocking collectives: 62.8 us -> 6.96 us
  other arithmetic: 55.9 us -> 71.8 us
    unnamed x25 -> x18, waiting for transfers between devices: 261 us -> 0.96 us
    unnamed x2 -> x1, blocking collectives: 62.8 us -> 6.96 us
    reduce_scatter x1 -> x2, waiting for transfers between devices: 96.5 us -> 128 us  [body(): lax.psum_scatter(whole, 'dp', scatter_dimension=0, tiled=True)[0]]
    concatenate x0 -> x26, local copies, waits for them, and re-layouts: none -> 26.8 us  [the longest x12 19.2 us: body(): jnp.concatenate((qkv_grad.reshape(width, -1), out_grad.T, up_grad, down_g...]
    unnamed x323 -> x297, local copies, waits for them, and re-layouts: 50.1 us -> 23.9 us
    reduce_scatter x2, waiting for transfers between devices: 56.5 us -> 40.4 us  [body(): lax.psum_scatter(ffn_back_rows(jnp.int32(0), rows_here * lax.axis_size('t...]
    reshape x8, local copies, waits for them, and re-layouts: 0.03 us -> 12.1 us  [the longest x2 8.64 us: body(): extra = extra.reshape(shares, -1, total_width)]
    concatenate x0 -> x2, other arithmetic: none -> 11.7 us  [body(): whole = jnp.concatenate((whole, extra), axis=1).astype(jnp.bfloat16)]
  transfers between devices with their start and end apart: 21 -> 18, of which waited for: 20 -> 17; matrix products, arithmetic and copies ran while one was open for 9% -> 15% of each run, Pallas kernels for 0% -> 0%
where the time goes in v1:
time: 765 us; the launch traced here: 756 us
  waiting for transfers between devices  469 us (61%)
  matrix products  116 us (15%)
  local copies, waits for them, and re-layouts  72 us (9%)
  other arithmetic  71.8 us (9%)
  between operations  17.1 us (2%)
    reduce_scatter x2, waiting for transfers between devices, body(): lax.psum_scatter(whole, 'dp', scatter_dimension=0, tiled=True)[0]  128 us
    reduce_scatter x2, waiting for transfers between devices, body(): lax.psum_scatter(attn_back_rows(jnp.int32(0), rows_here * lax.axis_size('...  56.7 us
    reduce_scatter x2, waiting for transfers between devices, body(): lax.psum_scatter(ffn_rows(jnp.int32(0), rows_here * lax.axis_size('tensor...  56.6 us
    reduce_scatter x2, waiting for transfers between devices, body(): lax.psum_scatter(attn_rows(jnp.int32(0), rows_here * lax.axis_size('tenso...  55.8 us
    reduce_scatter x2, waiting for transfers between devices, body(): lax.psum_scatter(ffn_back_rows(jnp.int32(0), rows_here * lax.axis_size('t...  40.4 us
    all_gather x2, waiting for transfers between devices, body(): lax.all_gather(grad_second.astype(jnp.bfloat16), 'tensor', axis=0, tiled=...  39.1 us
    all_gather x2, waiting for transfers between devices, body(): lax.all_gather(normed.astype(jnp.bfloat16), 'tensor', axis=0, tiled=True)  38.2 us
    all_gather x2, waiting for transfers between devices, body(): lax.all_gather(stream.astype(jnp.bfloat16), 'tensor', axis=0, tiled=True)  35.5 us
  transfers between devices with their start and end apart: 18, of which 17 were waited for; matrix products, arithmetic and copies ran while one was open for 15% of the time, Pallas kernels for 0%

profile of v1, /device:TPU:0, one launch (start us, length us, event | category | flops | bytes accessed | tf_op | source)
XLA Modules:
  0.0 756.5 jit_solution(5339576511689726657)
XLA Ops:
  15.4 16.6 %all-gather.9.cloned.1.call-done = bf16[1024,768]{1,0:T(8,128)(2,1)} async-done(((bf16[256,768]{1,0:T(8,128)(2,1)}), bf16[1024,768]{1,0:T(8,128)(2,1)}) %all-gather.9.cloned.1.call-update) | async-done | bytes 1572880 | tf_op jit(solution)/shard_map/all_gather | solution.py:140
  45.7 27.5 %reduce-scatter.12.cloned.1.call-done = bf16[256,768]{1,0:T(8,128)(2,1)} async-done(((bf16[1024,768]{1,0:T(8,128)(2,1)}), bf16[256,768]{1,0:T(8,128)(2,1)}) %reduce-scatter.12.cloned.1.call-update) | async-done | bytes 393232 | tf_op jit(solution)/shard_map/reduce_scatter | solution.py:159
  79.0 18.6 %all-gather.11.cloned.1.call-done = bf16[1024,768]{1,0:T(8,128)(2,1)} async-done(((bf16[256,768]{1,0:T(8,128)(2,1)}), bf16[1024,768]{1,0:T(8,128)(2,1)}) %all-gather.11.cloned.1.call-update) | async-done | bytes 1572880 | tf_op jit(solution)/shard_map/all_gather | solution.py:171
  97.6 11.6 %multiply_convert_fusion.5 = (bf16[1024,768]{1,0:T(8,128)(2,1)S(1)}, f32[1024,768]{1,0:T(8,128)}, f32[1024,768]{1,0:T(8,128)}) fusion(f32[768]{0:T(1024)S(1)} %get-tuple-element.205, bf16[1024,768]{1,0:T(8,128)(2,1)} %all-gather.11.cloned.1.call-done, bf16[2,768,768]{2,1,0:T(8,128)(2,1)} %param.40), kind=kOutput, calls=%fused_computation.52 | convolution fusion | flops 1259864064 | bytes 10619904 | tf_op jit(solution)/shard_map/dot_general | solution.py:173
  113.0 28.3 %reduce-scatter.14.cloned.1.call-done = bf16[256,768]{1,0:T(8,128)(2,1)} async-done(((bf16[1024,768]{1,0:T(8,128)(2,1)}), bf16[256,768]{1,0:T(8,128)(2,1)}) %reduce-scatter.14.cloned.1.call-update) | async-done | bytes 393232 | tf_op jit(solution)/shard_map/reduce_scatter | solution.py:187
  145.4 18.9 %all-gather.13.cloned.1.call-done = bf16[1024,768]{1,0:T(8,128)(2,1)} async-done(((bf16[256,768]{1,0:T(8,128)(2,1)}), bf16[1024,768]{1,0:T(8,128)(2,1)}) %all-gather.13.cloned.1.call-update) | async-done | bytes 1572880 | tf_op jit(solution)/shard_map/all_gather | solution.py:140
  178.4 28.3 %reduce-scatter.16.cloned.1.call-done = bf16[256,768]{1,0:T(8,128)(2,1)} async-done(((bf16[1024,768]{1,0:T(8,128)(2,1)}), bf16[256,768]{1,0:T(8,128)(2,1)}) %reduce-scatter.16.cloned.1.call-update) | async-done | bytes 393232 | tf_op jit(solution)/shard_map/reduce_scatter | solution.py:159
  211.7 19.6 %all-gather.15.cloned.1.call-done = bf16[1024,768]{1,0:T(8,128)(2,1)} async-done(((bf16[256,768]{1,0:T(8,128)(2,1)}), bf16[1024,768]{1,0:T(8,128)(2,1)}) %all-gather.15.cloned.1.call-update) | async-done | bytes 1572880 | tf_op jit(solution)/shard_map/all_gather | solution.py:171
  231.3 11.6 %multiply_convert_fusion.4 = (bf16[1024,768]{1,0:T(8,128)(2,1)S(1)}, f32[1024,768]{1,0:T(8,128)}, f32[1024,768]{1,0:T(8,128)}) fusion(f32[768]{0:T(1024)} %get-tuple-element.204, bf16[1024,768]{1,0:T(8,128)(2,1)} %all-gather.15.cloned.1.call-done, bf16[2,768,768]{2,1,0:T(8,128)(2,1)} %param.40), kind=kOutput, calls=%fused_computation.36 | convolution fusion | flops 1259864064 | bytes 10620928 | tf_op jit(solution)/shard_map/dot_general | solution.py:173
  246.7 28.3 %reduce-scatter.18.cloned.1.call-done = bf16[256,768]{1,0:T(8,128)(2,1)} async-done(((bf16[1024,768]{1,0:T(8,128)(2,1)}), bf16[256,768]{1,0:T(8,128)(2,1)}) %reduce-scatter.18.cloned.1.call-update) | async-done | bytes 393232 | tf_op jit(solution)/shard_map/reduce_scatter | solution.py:187
  282.0 19.8 %all-gather.17.cloned.1.call-done = bf16[1024,768]{1,0:T(8,128)(2,1)} async-done(((bf16[256,768]{1,0:T(8,128)(2,1)}), bf16[1024,768]{1,0:T(8,128)(2,1)}) %all-gather.17.cloned.1.call-update) | async-done | bytes 1572880 | tf_op jit(solution)/shard_map/all_gather | solution.py:233
  301.8 6.6 fusion.196
  312.2 28.3 %reduce-scatter.20.cloned.1.call-done = bf16[256,768]{1,0:T(8,128)(2,1)} async-done(((bf16[1024,768]{1,0:T(8,128)(2,1)}), bf16[256,768]{1,0:T(8,128)(2,1)}) %reduce-scatter.20.cloned.1.call-update) | async-done | bytes 393232 | tf_op jit(solution)/shard_map/reduce_scatter | solution.py:255
  349.7 17.5 %all-gather.19.cloned.1.call-done = bf16[1024,768]{1,0:T(8,128)(2,1)} async-done(((bf16[256,768]{1,0:T(8,128)(2,1)}), bf16[1024,768]{1,0:T(8,128)(2,1)}) %all-gather.19.cloned.1.call-update) | async-done | bytes 1572880 | tf_op jit(solution)/shard_map/all_gather | solution.py:263
  385.3 28.3 %reduce-scatter.22.cloned.1.call-done = bf16[256,768]{1,0:T(8,128)(2,1)} async-done(((bf16[1024,768]{1,0:T(8,128)(2,1)}), bf16[256,768]{1,0:T(8,128)(2,1)}) %reduce-scatter.22.cloned.1.call-update) | async-done | bytes 393232 | tf_op jit(solution)/shard_map/reduce_scatter | solution.py:302
  418.6 19.3 %all-gather.21.cloned.1.call-done = bf16[1024,768]{1,0:T(8,128)(2,1)} async-done(((bf16[256,768]{1,0:T(8,128)(2,1)}), bf16[1024,768]{1,0:T(8,128)(2,1)}) %all-gather.21.cloned.1.call-update) | async-done | bytes 1572880 | tf_op jit(solution)/shard_map/all_gather | solution.py:233
  437.9 6.6 fusion.198
  450.4 3.3 convolution_convert_fusion.6
  455.3 3.6 convolution_convert_fusion.7
  464.5 12.1 %reduce-scatter.24.cloned.1.call-done = bf16[256,768]{1,0:T(8,128)(2,1)} async-done(((bf16[1024,768]{1,0:T(8,128)(2,1)}), bf16[256,768]{1,0:T(8,128)(2,1)}) %reduce-scatter.24.cloned.1.call-update) | async-done | bytes 393232 | tf_op jit(solution)/shard_map/reduce_scatter | solution.py:255
  498.7 4.3 copy.110
  503.0 5.9 pad_maximum_fusion.1
  530.1 2.8 convolution_convert_fusion.8
  533.9 4.5 convolution_convert_fusion.9
  549.9 3.9 fusion.43
  553.7 3.2 concatenate.112
  560.8 4.3 copy.103
  565.1 5.9 pad_maximum_fusion
  572.9 31.7 %reduce-scatter.30.cloned.1.call-done = bf16[1,97,2304]{1,2,0:T(8,128)(2,1)} async-done(((bf16[8,97,2304]{1,2,0:T(8,128)(2,1)}), bf16[1,97,2304]{1,2,0:T(8,128)(2,1)}) %reduce-scatter.30.cloned.1.call-update) | async-done | bytes 446992 | tf_op jit(solution)/shard_map/reduce_scatter | solution.py:342
  606.6 28.5 %reduce-scatter.26.cloned.1.call-done = bf16[256,768]{1,0:T(8,128)(2,1)} async-done(((bf16[1024,768]{1,0:T(8,128)(2,1)}), bf16[256,768]{1,0:T(8,128)(2,1)}) %reduce-scatter.26.cloned.1.call-update) | async-done | bytes 393232 | tf_op jit(solution)/shard_map/reduce_scatter | solution.py:302
  637.0 96.8 %reduce-scatter.28.cloned.1.call-done = bf16[1,97,2304]{1,2,0:T(8,128)(2,1)} async-done(((bf16[8,97,2304]{1,2,0:T(8,128)(2,1)}), bf16[1,97,2304]{1,2,0:T(8,128)(2,1)}) %reduce-scatter.28.cloned.1.call-update) | async-done | bytes 446992 | tf_op jit(solution)/shard_map/reduce_scatter | solution.py:342
  735.7 7.0 all-reduce.6
  (538 shorter events, 186.3 us)
Async XLA Ops:
  7.2 24.8 %all-gather.9.cloned.1.call-start = ((), (), s32[]{:S(2)}) async-start(), calls=%async_computation.10 | async-start | bytes 1966080 | tf_op jit(solution)/shard_map/all_gather | solution.py:140
  7.9 65.4 %reduce-scatter.12.cloned.1.call-start = ((), (), s32[]{:S(2)}) async-start(), calls=%async_computation.11 | async-start | bytes 1966080 | tf_op jit(solution)/shard_map/reduce_scatter | solution.py:159
  43.1 34.7 %copy-start.126 = (bf16[3,64,512]{2,1,0:T(8,128)(2,1)}, bf16[3,64,512]{2,1,0:T(8,128)(2,1)S(1)}, u32[]{:S(2)}) copy-start(bf16[3,64,512]{2,1,0:T(8,128)(2,1)S(1)} %fusion.101) | copy-start | bytes 589828
  43.2 35.2 %copy-start.87 = (bf16[2,768]{1,0:T(2,128)(2,1)S(1)}, bf16[2,768]{1,0:T(2,128)(2,1)}, u32[]{:S(2)}) copy-start(bf16[2,768]{1,0:T(2,128)(2,1)} %param.41) | copy-start | bytes 9220
  45.0 52.6 %all-gather.11.cloned.1.call-start = ((), (), s32[]{:S(2)}) async-start(), calls=%async_computation.12 | async-start | bytes 1966080 | tf_op jit(solution)/shard_map/all_gather | solution.py:171
  45.7 97.3 %copy-start.69 = (f32[768]{0:T(1024)}, f32[768]{0:T(1024)S(1)}, u32[]{:S(2)}) copy-start(f32[768]{0:T(1024)S(1)} %get-tuple-element.195) | copy-start | bytes 9220
  45.7 160.9 %copy-start.55 = (f32[768]{0:T(1024)}, f32[768]{0:T(1024)S(1)}, u32[]{:S(2)}) copy-start(f32[768]{0:T(1024)S(1)} %get-tuple-element.295) | copy-start | bytes 9220
  74.5 66.8 %copy-start.64 = (f32[256]{0:T(256)}, f32[256]{0:T(256)S(1)}, u32[]{:S(2)}) copy-start(f32[256]{0:T(256)S(1)} %broadcast_multiply_fusion.3) | copy-start | bytes 3076
  75.8 33.4 %copy-start.90 = (f32[256]{0:T(256)}, f32[256]{0:T(256)S(1)}, u32[]{:S(2)}) copy-start(f32[256]{0:T(256)S(1)} %multiply_reduce_fusion.13) | copy-start | bytes 3076
  75.8 65.5 %copy-start.76 = (f32[256]{0:T(256)}, f32[256]{0:T(256)S(1)}, u32[]{:S(2)}) copy-start(f32[256]{0:T(256)S(1)} %fusion.160) | copy-start | bytes 3076
  77.8 63.5 %reduce-scatter.14.cloned.1.call-start = ((), (), s32[]{:S(2)}) async-start(), calls=%async_computation.13 | async-start | bytes 1966080 | tf_op jit(solution)/shard_map/reduce_scatter | solution.py:187
  112.9 51.4 %all-gather.13.cloned.1.call-start = ((), (), s32[]{:S(2)}) async-start(), calls=%async_computation.14 | async-start | bytes 1966080 | tf_op jit(solution)/shard_map/all_gather | solution.py:140
  144.6 62.1 %reduce-scatter.16.cloned.1.call-start = ((), (), s32[]{:S(2)}) async-start(), calls=%async_computation.15 | async-start | bytes 1966080 | tf_op jit(solution)/shard_map/reduce_scatter | solution.py:159
  178.3 52.9 %all-gather.15.cloned.1.call-start = ((), (), s32[]{:S(2)}) async-start(), calls=%async_computation.16 | async-start | bytes 1966080 | tf_op jit(solution)/shard_map/all_gather | solution.py:171
  211.4 63.5 %reduce-scatter.18.cloned.1.call-start = ((), (), s32[]{:S(2)}) async-start(), calls=%async_computation.17 | async-start | bytes 1966080 | tf_op jit(solution)/shard_map/reduce_scatter | solution.py:187
  246.6 55.1 %all-gather.17.cloned.1.call-start = ((), (), s32[]{:S(2)}) async-start(), calls=%async_computation.18 | async-start | bytes 1966080 | tf_op jit(solution)/shard_map/all_gather | solution.py:233
  281.9 58.5 %reduce-scatter.20.cloned.1.call-start = ((), (), s32[]{:S(2)}) async-start(), calls=%async_computation.19 | async-start | bytes 1966080 | tf_op jit(solution)/shard_map/reduce_scatter | solution.py:255
  312.1 55.1 %all-gather.19.cloned.1.call-start = ((), (), s32[]{:S(2)}) async-start(), calls=%async_computation.20 | async-start | bytes 1966080 | tf_op jit(solution)/shard_map/all_gather | solution.py:263
  347.4 66.2 %reduce-scatter.22.cloned.1.call-start = ((), (), s32[]{:S(2)}) async-start(), calls=%async_computation.21 | async-start | bytes 1966080 | tf_op jit(solution)/shard_map/reduce_scatter | solution.py:302
  382.6 31.0 %copy-start.5 = (f32[256,768]{1,0:T(8,128)S(1)}, f32[256,768]{1,0:T(8,128)}, u32[]{:S(2)}) copy-start(f32[256,768]{1,0:T(8,128)} %copy-done.4) | copy-start | bytes 2359300
  382.6 31.0 %copy-start.11 = (f32[256,768]{1,0:T(8,128)S(1)}, f32[256,768]{1,0:T(8,128)}, u32[]{:S(2)}) copy-start(f32[256,768]{1,0:T(8,128)} %copy-done.10) | copy-start | bytes 2359300
  382.6 31.0 %copy-start.56 = (f32[768]{0:T(1024)S(1)}, f32[768]{0:T(1024)}, u32[]{:S(2)}) copy-start(f32[768]{0:T(1024)} %copy-done.55) | copy-start | bytes 9220
  382.6 31.0 %copy-start.67 = (f32[256]{0:T(256)S(1)}, f32[256]{0:T(256)}, u32[]{:S(2)}) copy-start(f32[256]{0:T(256)} %copy-done.66) | copy-start | bytes 3076
  382.6 31.0 %copy-start.79 = (f32[256]{0:T(256)S(1)}, f32[256]{0:T(256)}, u32[]{:S(2)}) copy-start(f32[256]{0:T(256)} %copy-done.78) | copy-start | bytes 3076
  385.3 52.6 %all-gather.21.cloned.1.call-start = ((), (), s32[]{:S(2)}) async-start(), calls=%async_computation.22 | async-start | bytes 1966080 | tf_op jit(solution)/shard_map/all_gather | solution.py:233
  418.1 58.5 %reduce-scatter.24.cloned.1.call-start = ((), (), s32[]{:S(2)}) async-start(), calls=%async_computation.23 | async-start | bytes 1966080 | tf_op jit(solution)/shard_map/reduce_scatter | solution.py:255
  448.2 63.5 %all-gather.23.cloned.1.call-start = ((), (), s32[]{:S(2)}) async-start(), calls=%async_computation.24 | async-start | bytes 1966080 | tf_op jit(solution)/shard_map/all_gather | solution.py:263
  482.5 122.0 %reduce-scatter.30.cloned.1.call-start = ((), (), s32[]{:S(2)}) async-start(), calls=%async_computation.27 | async-start | bytes 5308416 | tf_op jit(solution)/shard_map/reduce_scatter | solution.py:342
  509.0 126.0 %reduce-scatter.26.cloned.1.call-start = ((), (), s32[]{:S(2)}) async-start(), calls=%async_computation.25 | async-start | bytes 1966080 | tf_op jit(solution)/shard_map/reduce_scatter | solution.py:302
  529.8 204.0 %reduce-scatter.28.cloned.1.call-start = ((), (), s32[]{:S(2)}) async-start(), calls=%async_computation.26 | async-start | bytes 5308416 | tf_op jit(solution)/shard_map/reduce_scatter | solution.py:342
  571.0 64.0 %copy-start.14 = (f32[256,768]{1,0:T(8,128)S(1)}, f32[256,768]{1,0:T(8,128)}, u32[]{:S(2)}) copy-start(f32[256,768]{1,0:T(8,128)} %copy-done.13) | copy-start | bytes 2359300
  571.0 64.0 %copy-start.89 = (f32[256]{0:T(256)S(1)}, f32[256]{0:T(256)}, u32[]{:S(2)}) copy-start(f32[256]{0:T(256)} %copy-done.88) | copy-start | bytes 3076
  (125 other events, 761.9 us)
Sparse Core Ops, SparseCore 0:
  9.6 22.3 all-gather.8
  45.1 28.1 reduce-scatter.11
  77.9 19.6 all-gather.10
  113.1 28.1 reduce-scatter.13
  144.7 19.6 all-gather.12
  178.5 28.1 reduce-scatter.15
  211.6 19.6 all-gather.14
  246.8 28.1 reduce-scatter.17
  282.1 19.6 all-gather.16
  312.2 28.1 reduce-scatter.19
  347.5 19.6 all-gather.18
  385.4 28.1 reduce-scatter.21
  418.2 19.6 all-gather.20
  448.3 28.2 reduce-scatter.23
  482.6 19.6 all-gather.22
  509.1 95.4 reduce-scatter.29
  607.1 27.8 reduce-scatter.25
  638.5 95.2 reduce-scatter.27

commit v2 on v0

v2 whole, which is shorter than its diff:
```python
from functools import partial

import jax
import jax.numpy as jnp
from jax import lax
from jax.experimental import pallas as pl
from jax.experimental.pallas import tpu as pltpu
from jax.sharding import PartitionSpec as P

HEAD_DIM = 64
SPAN = 256
GROUP = 4
LONGEST = 3
CHUNKS = 2
EPSILON = 1e-05
FAR = 1 << 20
F32 = jnp.float32
BF16 = jnp.bfloat16
MESH = pl.DeviceIdType.MESH
FWD_ATTN, FWD_FFN, BWD_FFN, BWD_ATTN = range(4)


def dot_nn(left, right):
    return lax.dot_general(left, right, (((1,), (0,)), ((), ())), preferred_element_type=F32)


def dot_nt(left, right):
    return lax.dot_general(left, right, (((1,), (1,)), ((), ())), preferred_element_type=F32)


def dot_tn(left, right):
    return lax.dot_general(left, right, (((0,), (0,)), ((), ())), preferred_element_type=F32)


def gelu_parts(value):
    cdf = 0.5 * (1.0 + lax.erf(value * 0.7071067811865476))
    density = jnp.exp(-0.5 * value * value) * 0.3989422804014327
    return value * cdf, cdf + value * density


def step_kernel(
    tokens_ref,
    cot_ref,
    vin_ref,
    doc_ref,
    pic_ref,
    wqkv_hbm,
    wout_hbm,
    wup_hbm,
    wdown_hbm,
    result_ref,
    tgrad_ref,
    vout_ref,
    grads_ref,
    wqkv,
    wout,
    wup,
    wdown,
    xr,
    q_all,
    k_all,
    v_all,
    prob,
    att,
    hr,
    act,
    slope,
    n_one,
    r_one,
    n_two,
    r_two,
    gf,
    ga,
    go,
    gq,
    gk,
    gv,
    gqkv,
    cur,
    mid,
    d0s,
    d0r,
    d1s,
    d1r,
    xsd,
    xrv,
    keep,
    w_sem,
    agx_s,
    agx_r,
    ags_s,
    ags_r,
    agf_s,
    agf_r,
    d0_s,
    d0_r,
    d1_s,
    d1_r,
    x_s,
    x_r,
):
    layers = vin_ref.shape[0]
    shard, width = tokens_ref.shape
    chunk = shard // CHUNKS
    heads_width = att.shape[2]
    window = LONGEST * SPAN
    hidden = wup.shape[2]
    me = lax.axis_index("tensor")
    row, col = me // 2, me % 2
    sib = row * 2 + (1 - col)
    cross = (1 - row) * 2 + col
    diag = (1 - row) * 2 + (1 - col)

    loads = []
    for place, (src, dst) in enumerate(
        ((wqkv_hbm, wqkv), (wout_hbm, wout), (wup_hbm, wup), (wdown_hbm, wdown))
    ):
        load = pltpu.make_async_copy(src, dst, w_sem.at[place])
        load.start()
        loads.append(load)

    barrier = pltpu.get_barrier_semaphore()
    for peer in (sib, cross):
        pl.semaphore_signal(barrier, inc=1, device_id={"tensor": peer}, device_id_type=MESH)
    pl.semaphore_wait(barrier, 2)

    def at_rows(owner, piece):
        return pl.ds(pl.multiple_of(owner * shard + piece * chunk, chunk), chunk)

    def span_rows(owner):
        return pl.ds(pl.multiple_of(owner * shard, shard), shard)

    def part(piece):
        return pl.ds(piece * chunk, chunk)

    def remote(src, dst, send, recv, peer):
        return pltpu.make_async_remote_copy(
            src_ref=src,
            dst_ref=dst,
            send_sem=send,
            recv_sem=recv,
            device_id={"tensor": peer},
            device_id_type=MESH,
        )

    def ag_copy(kind, phase, layer, piece, buf):
        owner, peer, send, recv = {
            "x": (me, cross, agx_s, agx_r),
            "s": (me, sib, ags_s, ags_r),
            "f": (cross, sib, agf_s, agf_r),
        }[kind]
        view = buf.at[at_rows(owner, piece)]
        return remote(view, view, send.at[phase, layer, piece], recv.at[phase, layer, piece], peer)

    def ag_recv(kind, phase, layer, piece, buf):
        owner, peer, send, recv = {
            "x": (cross, cross, agx_s, agx_r),
            "s": (sib, sib, ags_s, ags_r),
            "f": (diag, sib, agf_s, agf_r),
        }[kind]
        view = buf.at[at_rows(owner, piece)]
        return remote(view, view, send.at[phase, layer, piece], recv.at[phase, layer, piece], peer)

    def ag_send(phase, layer, piece, buf):
        ag_copy("x", phase, layer, piece, buf).start()
        ag_copy("s", phase, layer, piece, buf).start()

    def ag_forward(phase, layer, piece, buf):
        ag_recv("x", phase, layer, piece, buf).wait_recv()
        ag_copy("f", phase, layer, piece, buf).start()

    def ag_done(phase, layer, buf):
        for piece in range(CHUNKS):
            for kind in "xsf":
                ag_copy(kind, phase, layer, piece, buf).wait_send()

    def rs_copy(kind, phase, layer, piece):
        src, dst, send, recv, peer = {
            "d0": (d0s, d0r, d0_s, d0_r, sib),
            "d1": (d1s, d1r, d1_s, d1_r, sib),
            "x": (xsd, xrv, x_s, x_r, cross),
        }[kind]
        return remote(
            src.at[piece],
            dst.at[piece],
            send.at[phase, layer, piece],
            recv.at[phase, layer, piece],
            peer,
        )

    def rs_diag(phase, layer, piece, value):
        d0s[piece] = value.astype(BF16)
        rs_copy("d0", phase, layer, piece).start()

    def rs_cross(phase, layer, piece, value):
        rs_copy("d0", phase, layer, piece).wait_recv()
        xsd[piece] = (value + d0r[piece].astype(F32)).astype(BF16)
        rs_copy("x", phase, layer, piece).start()

    def rs_sib(phase, layer, piece, value):
        d1s[piece] = value.astype(BF16)
        rs_copy("d1", phase, layer, piece).start()

    def rs_final(phase, layer, piece):
        rs_copy("d1", phase, layer, piece).wait_recv()
        rs_copy("x", phase, layer, piece).wait_recv()
        total = keep[piece] + d1r[piece].astype(F32) + xrv[piece].astype(F32)
        for kind in ("d0", "d1", "x"):
            rs_copy(kind, phase, layer, piece).wait_send()
        return total

    def vec(layer, place):
        return vin_ref[layer, pl.ds(place, 1), :]

    def norm_forward(layer, piece, value, gain, shift, normed, inverse):
        centered = value - jnp.mean(value, axis=-1, keepdims=True)
        scale = lax.rsqrt(jnp.mean(centered * centered, axis=-1, keepdims=True) + EPSILON)
        unit = centered * scale
        normed[layer, part(piece), :] = unit
        inverse[layer, part(piece), :] = scale
        return unit * vec(layer, gain) + vec(layer, shift)

    def norm_backward(layer, piece, grad, gain, normed, inverse, rows):
        unit = normed[layer, part(piece), :]
        scale = inverse[layer, part(piece), :]
        scaled = grad * vec(layer, gain)
        out = scale * (
            scaled
            - jnp.mean(scaled, axis=-1, keepdims=True)
            - unit * jnp.mean(scaled * unit, axis=-1, keepdims=True)
        )
        gain_row, shift_row, bias_row = rows
        for place, term in ((gain_row, grad * unit), (shift_row, grad), (bias_row, out)):
            vout_ref[layer, pl.ds(place, 1), :] += jnp.sum(term, axis=0, keepdims=True)
        return out

    groups = []
    for begin in range(0, heads_width, 128):
        wide = min(128, heads_width - begin)
        groups.append((begin, wide, range(begin // HEAD_DIM, (begin + wide) // HEAD_DIM)))

    def only_head(value, begin, head):
        if value.shape[1] == HEAD_DIM:
            return value
        lane = lax.broadcasted_iota(jnp.int32, value.shape, 1)
        low = head * HEAD_DIM - begin
        return jnp.where((lane >= low) & (lane < low + HEAD_DIM), value, jnp.zeros_like(value))

    def window_of(span):
        return pl.ds(pl.multiple_of((span // LONGEST) * SPAN, SPAN), window)

    def attend(layer, span):
        rows = span_rows(span)
        keys = window_of(span)
        query_pos = span * SPAN + lax.broadcasted_iota(jnp.int32, (SPAN, 1), 0)
        picture = jnp.full((SPAN, 1), pic_ref[span], jnp.int32) == 1
        limit = jnp.where(picture, span * SPAN + SPAN - 1, query_pos)
        key_pos = (span // LONGEST) * SPAN + lax.broadcasted_iota(jnp.int32, (1, window), 1)
        first = jnp.full((1, window), doc_ref[span] * SPAN, jnp.int32)
        key_pos = jnp.where(key_pos >= first, key_pos, FAR)
        allowed = key_pos <= limit
        for begin, wide, heads in groups:
            cols = pl.ds(begin, wide)
            q_here = q_all[layer, rows, cols]
            k_here = k_all[layer, keys, cols]
            v_here = v_all[layer, keys, cols]
            total = jnp.zeros((SPAN, wide), F32)
            for head in heads:
                scores = dot_nt(only_head(q_here, begin, head), k_here)
                scores = jnp.where(allowed, scores, -1e30)
                raised = jnp.exp(scores - jnp.max(scores, axis=-1, keepdims=True))
                share = raised * (1.0 / jnp.sum(raised, axis=-1, keepdims=True))
                share = share.astype(BF16)
                prob[layer, span, head] = share
                total = total + dot_nn(share, only_head(v_here, begin, head))
            att[layer, rows, cols] = total.astype(BF16)

    def attend_back(layer, span):
        rows = span_rows(span)
        keys = window_of(span)
        for begin, wide, heads in groups:
            cols = pl.ds(begin, wide)
            q_here = q_all[layer, rows, cols]
            k_here = k_all[layer, keys, cols]
            v_here = v_all[layer, keys, cols]
            go_here = go[rows, cols]
            mixed = go_here.astype(F32) * att[layer, rows, cols].astype(F32)
            total = jnp.zeros((SPAN, wide), F32)
            key_total = gk[keys, cols]
            value_total = gv[keys, cols]
            for head in heads:
                go_head = only_head(go_here, begin, head)
                inner = jnp.sum(only_head(mixed, begin, head), axis=-1, keepdims=True)
                gp = dot_nt(go_head, v_here)
                share = prob[layer, span, head]
                gs = (share.astype(F32) * (gp - inner)).astype(BF16)
                total = total + dot_nn(gs, only_head(k_here, begin, head))
                key_total = key_total + dot_tn(gs, only_head(q_here, begin, head))
                value_total = value_total + dot_tn(share, go_head)
            gk[keys, cols] = key_total
            gv[keys, cols] = value_total
            gq[rows, cols] = total * 0.125

    def project(layer, owner):
        rows = span_rows(owner)
        out = dot_nn(xr[layer, rows, :], wqkv[layer])
        bias = vec(layer, 7)
        q_all[layer, rows, :] = (
            (out[:, :heads_width] + bias[:, :heads_width]) * 0.125
        ).astype(BF16)
        k_all[layer, rows, :] = out[:, heads_width : 2 * heads_width].astype(BF16)
        v_all[layer, rows, :] = (
            out[:, 2 * heads_width :] + bias[:, heads_width : 2 * heads_width]
        ).astype(BF16)

    def two(buf, first, second, piece):
        return jnp.concatenate(
            (buf[at_rows(first, piece), :], buf[at_rows(second, piece), :]), axis=0
        )

    def ffn_rows(layer, first, second, piece):
        pre = dot_nn(two(hr.at[layer], first, second, piece), wup[layer]) + vec(layer, 6)
        value, grad = gelu_parts(pre)
        value, grad = value.astype(BF16), grad.astype(BF16)
        for place, owner in enumerate((first, second)):
            rows = at_rows(owner, piece)
            act[layer, rows, :] = value[place * chunk : (place + 1) * chunk]
            slope[layer, rows, :] = grad[place * chunk : (place + 1) * chunk]
        out = dot_nn(value, wdown[layer])
        return out[:chunk], out[chunk:]

    def ffn_back_rows(layer, first, second, piece):
        gu = dot_nt(two(gf, first, second, piece), wdown[layer])
        gpre = (gu * two(slope.at[layer], first, second, piece).astype(F32)).astype(BF16)
        for place, owner in enumerate((first, second)):
            slope[layer, at_rows(owner, piece), :] = gpre[place * chunk : (place + 1) * chunk]
        out = dot_nt(gpre, wup[layer])
        return out[:chunk], out[chunk:]

    def ffn_phase(phase, layer, buf, rows_of):
        for piece in range(CHUNKS):
            ag_recv("s", phase, layer, piece, buf).wait_recv()
            own_part, sib_part = rows_of(layer, me, sib, piece)
            rs_sib(phase, layer, piece, sib_part)
            keep[piece] = own_part
        for piece in range(CHUNKS):
            ag_forward(phase, layer, piece, buf)
            ag_recv("f", phase, layer, piece, buf).wait_recv()
            cross_part, diag_part = rows_of(layer, cross, diag, piece)
            rs_diag(phase, layer, piece, diag_part)
            rs_cross(phase, layer, piece, cross_part)
        ag_done(phase, layer, buf)

    def weight_grad(layer, left, right, begin, wide):
        def block(place, carry):
            cols = pl.ds(pl.multiple_of(place * 256, 256), 256)
            grads_ref[layer, cols, pl.ds(begin, wide)] = dot_tn(left[:, cols], right[...]).astype(
                BF16
            )
            return carry

        lax.fori_loop(0, width // 256, block, 0)

    vout_ref[...] = jnp.zeros_like(vout_ref)
    cur[...] = tokens_ref[...].astype(F32)

    def forward(layer, carry):
        here = xr.at[layer]
        for piece in range(CHUNKS):
            xr[layer, at_rows(me, piece), :] = cur[part(piece), :].astype(BF16)
            ag_send(FWD_ATTN, layer, piece, here)

        @pl.when(layer == 0)
        def _():
            loads[0].wait()
            loads[1].wait()

        project(layer, me)
        for piece in range(CHUNKS):
            ag_recv("s", FWD_ATTN, layer, piece, here).wait_recv()
        project(layer, sib)

        @pl.when(layer == 0)
        def _():
            loads[2].wait()
            loads[3].wait()

        for piece in range(CHUNKS):
            ag_forward(FWD_ATTN, layer, piece, here)
        project(layer, cross)
        for piece in range(CHUNKS):
            ag_recv("f", FWD_ATTN, layer, piece, here).wait_recv()
        project(layer, diag)
        for owner, send in ((diag, rs_diag), (cross, rs_cross), (sib, rs_sib), (me, None)):
            attend(layer, owner)
            out = dot_nn(att[layer, span_rows(owner), :], wout[layer])
            for piece in range(CHUNKS):
                value = out[piece * chunk : (piece + 1) * chunk]
                if send is None:
                    keep[piece] = value
                else:
                    send(FWD_ATTN, layer, piece, value)
        ag_done(FWD_ATTN, layer, here)
        there = hr.at[layer]
        for piece in range(CHUNKS):
            value = cur[part(piece), :] + rs_final(FWD_ATTN, layer, piece) + vec(layer, 0)
            value = norm_forward(layer, piece, value, 4, 1, n_one, r_one)
            mid[part(piece), :] = value
            hr[layer, at_rows(me, piece), :] = value.astype(BF16)
            ag_send(FWD_FFN, layer, piece, there)
        ffn_phase(FWD_FFN, layer, there, ffn_rows)
        for piece in range(CHUNKS):
            value = mid[part(piece), :] + rs_final(FWD_FFN, layer, piece) + vec(layer, 2)
            cur[part(piece), :] = norm_forward(layer, piece, value, 5, 3, n_two, r_two)
        return carry

    lax.fori_loop(0, layers, forward, 0)
    result_ref[...] = cur[...]

    cur[...] = cot_ref[...].astype(F32)

    def backward(step, carry):
        layer = layers - 1 - step
        for piece in range(CHUNKS):
            grad = norm_backward(layer, piece, cur[part(piece), :], 5, n_two, r_two, (5, 3, 2))
            mid[part(piece), :] = grad
            gf[at_rows(me, piece), :] = grad.astype(BF16)
            ag_send(BWD_FFN, layer, piece, gf)
        ffn_phase(BWD_FFN, layer, gf, ffn_back_rows)
        weight_grad(layer, gf, act.at[layer], hidden, hidden)
        for piece in range(CHUNKS):
            grad = mid[part(piece), :] + rs_final(BWD_FFN, layer, piece)
            grad = norm_backward(layer, piece, grad, 4, n_one, r_one, (4, 1, 0))
            cur[part(piece), :] = grad
            ga[at_rows(me, piece), :] = grad.astype(BF16)
            ag_send(BWD_ATTN, layer, piece, ga)
        weight_grad(layer, hr.at[layer], slope.at[layer], 0, hidden)
        vout_ref[layer, pl.ds(6, 1), :] = jnp.sum(
            slope[layer].astype(F32), axis=0, keepdims=True
        )
        gk[...] = jnp.zeros_like(gk)
        gv[...] = jnp.zeros_like(gv)

        def heads_grad(owner):
            rows = span_rows(owner)
            go[rows, :] = dot_nt(ga[rows, :], wout[layer]).astype(BF16)
            attend_back(layer, owner)

        heads_grad(me)
        for piece in range(CHUNKS):
            ag_recv("s", BWD_ATTN, layer, piece, ga).wait_recv()
        heads_grad(sib)
        for piece in range(CHUNKS):
            ag_forward(BWD_ATTN, layer, piece, ga)
        heads_grad(cross)
        for piece in range(CHUNKS):
            ag_recv("f", BWD_ATTN, layer, piece, ga).wait_recv()
        heads_grad(diag)
        for owner, send in ((diag, rs_diag), (cross, rs_cross), (sib, rs_sib), (me, None)):
            rows = span_rows(owner)
            joined = jnp.concatenate((gq[rows, :], gk[rows, :], gv[rows, :]), axis=1).astype(BF16)
            gqkv[rows, :] = joined
            out = dot_nt(joined, wqkv[layer])
            for piece in range(CHUNKS):
                value = out[piece * chunk : (piece + 1) * chunk]
                if send is None:
                    keep[piece] = value
                else:
                    send(BWD_ATTN, layer, piece, value)
        ag_done(BWD_ATTN, layer, ga)
        weight_grad(layer, xr.at[layer], gqkv, 2 * hidden, 3 * heads_width)
        weight_grad(layer, ga, att.at[layer], 2 * hidden + 3 * heads_width, heads_width)
        sums = jnp.sum(gqkv[...].astype(F32), axis=0, keepdims=True)
        vout_ref[layer, pl.ds(7, 1), pl.ds(0, heads_width)] = sums[:, :heads_width]
        vout_ref[layer, pl.ds(7, 1), pl.ds(heads_width, heads_width)] = sums[:, 2 * heads_width :]
        for piece in range(CHUNKS):
            cur[part(piece), :] = cur[part(piece), :] + rs_final(BWD_ATTN, layer, piece)
        return carry

    lax.fori_loop(0, layers, backward, 0)
    tgrad_ref[...] = cur[...]


def body(
    tokens,
    qkv_weight,
    qv_bias,
    out_weight,
    up_weight,
    up_bias,
    down_weight,
    out_bias,
    norm_gain,
    doc_start,
    picture,
    cotangent,
):
    layers, width, _, heads_width = qkv_weight.shape
    shard = tokens.shape[0]
    seq = shard * GROUP
    hidden = up_weight.shape[2]
    spans = seq // SPAN
    heads = heads_width // HEAD_DIM
    total_width = 4 * heads_width + 2 * hidden
    chunk = shard // CHUNKS
    wide = max(hidden, width)
    vin = jnp.concatenate(
        (
            out_bias,
            norm_gain,
            up_bias[:, None, :],
            jnp.pad(
                qv_bias.reshape(layers, 1, 2 * heads_width),
                ((0, 0), (0, 0), (0, wide - 2 * heads_width)),
            ),
        ),
        axis=1,
    ).astype(F32)
    vmem = partial(pl.BlockSpec, memory_space=pltpu.VMEM)
    smem = partial(pl.BlockSpec, memory_space=pltpu.SMEM)
    anywhere = partial(pl.BlockSpec, memory_space=pl.ANY)
    sems = pltpu.SemaphoreType.DMA((4, layers, CHUNKS))
    result, tokens_grad, vout, grads = pl.pallas_call(
        step_kernel,
        name="encoder_step",
        out_shape=(
            jax.ShapeDtypeStruct((shard, width), F32),
            jax.ShapeDtypeStruct((shard, width), F32),
            jax.ShapeDtypeStruct((layers, 8, wide), F32),
            jax.ShapeDtypeStruct((layers, width, total_width), BF16),
        ),
        in_specs=[vmem(), vmem(), vmem(), smem(), smem()] + [anywhere()] * 4,
        out_specs=(vmem(), vmem(), vmem(), vmem()),
        scratch_shapes=[
            pltpu.VMEM((layers, width, 3 * heads_width), BF16),
            pltpu.VMEM(out_weight.shape, BF16),
            pltpu.VMEM(up_weight.shape, BF16),
            pltpu.VMEM(down_weight.shape, BF16),
            pltpu.VMEM((layers, seq, width), BF16),
            pltpu.VMEM((layers, seq, heads_width), BF16),
            pltpu.VMEM((layers, seq, heads_width), BF16),
            pltpu.VMEM((layers, seq, heads_width), BF16),
            pltpu.VMEM((layers, spans, heads, SPAN, LONGEST * SPAN), BF16),
            pltpu.VMEM((layers, seq, heads_width), BF16),
            pltpu.VMEM((layers, seq, width), BF16),
            pltpu.VMEM((layers, seq, hidden), BF16),
            pltpu.VMEM((layers, seq, hidden), BF16),
            pltpu.VMEM((layers, shard, width), F32),
            pltpu.VMEM((layers, shard, 1), F32),
            pltpu.VMEM((layers, shard, width), F32),
            pltpu.VMEM((layers, shard, 1), F32),
            pltpu.VMEM((seq, width), BF16),
            pltpu.VMEM((seq, width), BF16),
            pltpu.VMEM((seq, heads_width), BF16),
            pltpu.VMEM((seq, heads_width), F32),
            pltpu.VMEM((seq, heads_width), F32),
            pltpu.VMEM((seq, heads_width), F32),
            pltpu.VMEM((seq, 3 * heads_width), BF16),
            pltpu.VMEM((shard, width), F32),
            pltpu.VMEM((shard, width), F32),
        ]
        + [pltpu.VMEM((CHUNKS, chunk, width), BF16)] * 6
        + [pltpu.VMEM((CHUNKS, chunk, width), F32), pltpu.SemaphoreType.DMA((4,))]
        + [sems] * 12,
        compiler_params=pltpu.CompilerParams(
            collective_id=0, has_side_effects=True, vmem_limit_bytes=67043328
        ),
    )(
        tokens,
        cotangent,
        vin,
        doc_start,
        picture,
        qkv_weight.reshape(layers, width, 3 * heads_width),
        out_weight,
        up_weight,
        down_weight,
    )
    shares = lax.axis_size("dp")
    rows_each = width // shares
    head_each = heads_width // shares
    up_each = hidden // shares
    place = lax.axis_index("dp")
    summed = [
        lax.psum_scatter(grads[layer], "dp", scatter_dimension=0, tiled=True).astype(F32)
        for layer in range(layers)
    ]
    main = jnp.stack(summed)
    qkv_part = main[:, :, 2 * hidden : 2 * hidden + 3 * heads_width].reshape(
        layers, rows_each, 3, heads_width
    )
    out_part = main[:, :, 2 * hidden + 3 * heads_width :].transpose(0, 2, 1)
    up_part = main[:, :, :hidden]
    down_part = main[:, :, hidden : 2 * hidden].transpose(0, 2, 1)
    vector_sum = lax.psum(vout[:, :6], ("dp", "tensor"))
    bias_sum = lax.psum(vout[:, 6:], "dp")
    fine = width // (shares * GROUP)
    vector_sum = lax.dynamic_slice_in_dim(
        vector_sum, place * rows_each + lax.axis_index("tensor") * fine, fine, 2
    )
    head_sum = bias_sum[:, 1, : 2 * heads_width].reshape(layers, 2, heads_width)
    return (
        result,
        tokens_grad,
        qkv_part,
        lax.dynamic_slice_in_dim(head_sum, place * head_each, head_each, 2),
        out_part,
        up_part,
        lax.dynamic_slice_in_dim(bias_sum[:, 0, :hidden], place * up_each, up_each, 1),
        down_part,
        vector_sum[:, :4],
        vector_sum[:, 4:],
    )


def solution(mesh):
    return jax.shard_map(
        body,
        mesh=mesh,
        in_specs=(
            P(("dp", "tensor"), None),
            P(None, None, None, "tensor"),
            P(None, None, "tensor"),
            P(None, "tensor", None),
            P(None, None, "tensor"),
            P(None, "tensor"),
            P(None, "tensor", None),
            P(),
            P(),
            P("dp"),
            P("dp"),
            P(("dp", "tensor"), None),
        ),
        out_specs=(
            P(("dp", "tensor"), None),
            P(("dp", "tensor"), None),
            P(None, "dp", None, "tensor"),
            P(None, None, ("tensor", "dp")),
            P(None, "tensor", "dp"),
            P(None, "dp", "tensor"),
            P(None, ("tensor", "dp")),
            P(None, "tensor", "dp"),
            P(None, None, ("dp", "tensor")),
            P(None, None, ("dp", "tensor")),
        ),
        check_vma=False,
    )
```

time: 1030 us -> 384 us (0.37)
  waiting for transfers between devices: 713 us -> 84.1 us
  Pallas kernels: 0 us -> 187 us
  matrix products: 110 us -> 0 us
  other arithmetic: 55.9 us -> 2.83 us
  local copies, waits for them, and re-layouts: 63.2 us -> 19.7 us
  blocking collectives: 62.8 us -> 76.2 us
    unnamed x25 -> x2, waiting for transfers between devices: 261 us -> 0.71 us
    reduce_scatter x9 -> x2, waiting for transfers between devices: 322 us -> 83.4 us  [body(): lax.psum_scatter(grads[layer], 'dp', scatter_dimension=0, tiled=True)]
    pallas_call x0 -> x1, Pallas kernels: none -> 187 us  [body(): pl.pallas_call(step_kernel, name='encoder_step', out_shape=(jax.ShapeDtyp...]
    all_gather x8 -> x0, waiting for transfers between devices: 130 us -> none  [the longest x2 39.4 us: body(): lax.all_gather(grad_second.astype(jnp.bfloat16), 'tensor', axis=0, tiled=...]
    dot_general x45 -> x0, matrix products: 102 us -> none  [the longest x2 23.4 us: body(): jnp.dot(normed_rows, up_weight[layer_idx], preferred_element_type=jnp.flo...]
    psum x0 -> x2, blocking collectives: none -> 76.2 us  [the longest x1 38.3 us: body(): bias_sum = lax.psum(vout[:, 6:], 'dp')]
    unnamed x2 -> x0, blocking collectives: 62.8 us -> none
    unnamed x323 -> x14, local copies, waits for them, and re-layouts: 50.1 us -> 3.69 us
  transfers between devices with their start and end apart: 21 -> 2, of which waited for: 20 -> 2; matrix products, arithmetic and copies ran while one was open for 9% -> 1% of each run, Pallas kernels for 0% -> 0%
where the time goes in v2:
time: 384 us
  Pallas kernels  187 us (49%)
  waiting for transfers between devices  84.1 us (22%)
  blocking collectives  76.2 us (20%)
  local copies, waits for them, and re-layouts  19.7 us (5%)
  between operations  14.1 us (4%)
    pallas_call x1, Pallas kernels, body(): pl.pallas_call(step_kernel, name='encoder_step', out_shape=(jax.ShapeDtyp...  187 us
    reduce_scatter x2, waiting for transfers between devices, body(): lax.psum_scatter(grads[layer], 'dp', scatter_dimension=0, tiled=True)  83.4 us
    psum x1, blocking collectives, body(): bias_sum = lax.psum(vout[:, 6:], 'dp')  38.3 us
    psum x1, blocking collectives, body(): vector_sum = lax.psum(vout[:, :6], ('dp', 'tensor'))  37.9 us
  transfers between devices with their start and end apart: 2, of which 2 were waited for; matrix products, arithmetic and copies ran while one was open for 1% of the time, Pallas kernels for 0%

profile of v2, /device:TPU:0, one launch (start us, length us, event | category | flops | bytes accessed | tf_op | source)
XLA Modules:
  0.0 384.0 jit_solution(1271503507453652924)
XLA Ops:
  7.2 0.0 copy-start.4
  7.2 0.0 copy-start.3
  7.2 0.0 reduce-scatter.3.cloned.1.call-start
  7.2 0.8 reshape.33
  8.0 0.7 copy.26
  8.7 3.9 %copy.27.wqkv_hbm = bf16[2,768,576]{2,1,0:T(8,128)(2,1)} copy(bf16[2,768,576]{1,2,0:T(8,128)(2,1)} %bitcast.16) | data formatting | bytes 3538944 | tf_op jit(solution)/shard_map/reshape | solution.py:574
  12.6 0.0 copy-done.4
  12.6 0.0 copy-done.3
  12.6 0.7 fusion.2.vin_ref
  13.3 187.1 %encoder_step.1 = (f32[256,768]{1,0:T(8,128)}, f32[256,768]{1,0:T(8,128)}, f32[2,8,768]{2,1,0:T(8,128)}, bf16[2,768,2304]{2,1,0:T(8,128)(2,1)}) custom-call(bf16[256,768]{1,0:T(8,128)(2,1)} %tokens_ref.1, bf16[256,768]{1,0:T(8,128)(2,1)} %cot_ref.1, f32[2,8,768]{2,1,0:T(8,128)} %fusion.2.vin_ref, s32[4]{0:T(128)} %doc_ref.1, s32[4]{0:T(128)} %pic_ref.1, ...), custom_call_target="tpu_custom_call" | custom-call | tf_op jit(solution)/shard_map/encoder_step/pallas_call | solution.py:523
  200.4 6.5 %slice_bitcast_fusion.1 = (bf16[768,2304]{1,0:T(8,128)(2,1)}, bf16[768,2304]{1,0:T(8,128)(2,1)}) fusion(bf16[2,768,2304]{2,1,0:T(8,128)(2,1)} %get-tuple-element.16), kind=kLoop, calls=%fused_computation.1 | loop fusion | bytes 14155776 | tf_op jit(solution)/shard_map/squeeze | solution.py:585
  206.8 0.0 reduce-scatter.3.cloned.1.call-update
  206.9 0.0 reduce-scatter.5.cloned.1.call-start
  206.9 0.7 reduce-scatter.5.cloned.1.call-update
  207.6 0.0 copy-done.2
  207.7 38.3 %psum.14 = f32[2,2,768]{2,1,0:T(2,128)S(1)} all-reduce(f32[2,2,768]{2,1,0:T(2,128)S(1)} %slice.39), channel_id=1, replica_groups=mesh['dp'=8,'tensor'=4] {'dp'}, use_global_device_ids=true, to_apply=%region_2.3 | all-reduce | flops 3072 | bytes 24576 | tf_op jit(solution)/shard_map/psum | solution.py:596
  246.0 0.1 reshape_squeeze.3
  246.1 37.9 %psum.15 = f32[2,6,768]{2,1,0:T(8,128)S(1)} all-reduce(f32[2,6,768]{2,1,0:T(8,128)S(1)} %bitcast.21), channel_id=1, replica_groups=mesh['dp'=8,'tensor'=4] {'dp','tensor'}, use_global_device_ids=true, to_apply=%region_3.4 | all-reduce | flops 9216 | bytes 73728 | tf_op jit(solution)/shard_map/psum | solution.py:595
  284.0 0.6 constant_dynamic-slice_fusion.2
  284.6 0.7 constant_dynamic-slice_fusion.3
  285.2 0.7 constant_dynamic-slice_fusion.1
  285.9 0.7 constant_dynamic-slice_fusion
  286.6 0.9 reduce-scatter.3.cloned.1.call-done
  287.5 82.4 %reduce-scatter.5.cloned.1.call-done = bf16[96,2304]{1,0:T(8,128)(2,1)} async-done(((bf16[768,2304]{1,0:T(8,128)(2,1)}), bf16[96,2304]{1,0:T(8,128)(2,1)}) %reduce-scatter.5.cloned.1.call-update) | async-done | bytes 442384 | tf_op jit(solution)/shard_map/reduce_scatter | solution.py:585
  369.9 0.9 convert_bitcast_fusion
  370.8 1.3 maximum_convert_fusion
  372.2 1.1 slice_bitcast_fusion.2
  373.3 0.8 copy.30
  374.1 0.2 copy.28
  374.3 1.1 copy.29
  375.4 0.9 copy.33
  376.3 0.9 copy.34
  (9 shorter events, 0.1 us)
Async XLA Ops:
  7.2 5.5 %copy-start.4 = (bf16[2,2,768]{2,1,0:T(2,128)(2,1)S(1)}, bf16[2,2,768]{2,1,0:T(2,128)(2,1)}, u32[]{:S(2)}) copy-start(bf16[2,2,768]{2,1,0:T(2,128)(2,1)} %param.20) | copy-start | bytes 18436
  7.2 5.5 %copy-start.3 = (bf16[2,4,768]{2,1,0:T(4,128)(2,1)S(1)}, bf16[2,4,768]{2,1,0:T(4,128)(2,1)}, u32[]{:S(2)}) copy-start(bf16[2,4,768]{2,1,0:T(4,128)(2,1)} %param.19) | copy-start | bytes 36868
  7.2 280.3 %reduce-scatter.3.cloned.1.call-start = ((), (), s32[]{:S(2)}) async-start(), calls=%async_computation.2 | async-start | bytes 3981312 | tf_op jit(solution)/shard_map/reduce_scatter | solution.py:585
  206.9 0.8 copy-start.2
  206.9 163.1 %reduce-scatter.5.cloned.1.call-start = ((), (), s32[]{:S(2)}) async-start(), calls=%async_computation.3 | async-start | bytes 3981312 | tf_op jit(solution)/shard_map/reduce_scatter | solution.py:585
  372.2 3.2 copy-start.1
  373.3 3.0 copy-start
Sparse Core Ops, SparseCore 0:
  207.0 80.4 reduce-scatter.2
  291.1 78.7 reduce-scatter.4

commit v3 on v2

--- a/solution.py
+++ b/solution.py
@@ -13,7 +13,9 @@
 LONGEST = 3
 CHUNKS = 2
 EPSILON = 1e-05
-FAR = 1 << 20
+BEYOND = 1 << 20
+NEAR, FAR_SIDE = 2, 4
+NEAR_ORDER = (1, 0, 2, None)
 F32 = jnp.float32
 BF16 = jnp.bfloat16
 MESH = pl.DeviceIdType.MESH
@@ -38,69 +40,80 @@
     return value * cdf, cdf + value * density
 
 
-def step_kernel(
-    tokens_ref,
-    cot_ref,
-    vin_ref,
-    doc_ref,
-    pic_ref,
-    wqkv_hbm,
-    wout_hbm,
-    wup_hbm,
-    wdown_hbm,
-    result_ref,
-    tgrad_ref,
-    vout_ref,
-    grads_ref,
-    wqkv,
-    wout,
-    wup,
-    wdown,
-    xr,
-    q_all,
-    k_all,
-    v_all,
-    prob,
-    att,
-    hr,
-    act,
-    slope,
-    n_one,
-    r_one,
-    n_two,
-    r_two,
-    gf,
-    ga,
-    go,
-    gq,
-    gk,
-    gv,
-    gqkv,
-    cur,
-    mid,
-    d0s,
-    d0r,
-    d1s,
-    d1r,
-    xsd,
-    xrv,
-    keep,
-    w_sem,
-    agx_s,
-    agx_r,
-    ags_s,
-    ags_r,
-    agf_s,
-    agf_r,
-    d0_s,
-    d0_r,
-    d1_s,
-    d1_r,
-    x_s,
-    x_r,
-):
-    layers = vin_ref.shape[0]
-    shard, width = tokens_ref.shape
+def step_kernel(inside, *refs):
+    (
+        tokens_hbm,
+        cot_hbm,
+        obias_ref,
+        gain_ref,
+        ubias_ref,
+        hbias_ref,
+        doc_ref,
+        pic_ref,
+        wqkv_hbm,
+        wout_hbm,
+        wup_hbm,
+        wdown_hbm,
+        result_hbm,
+        tgrad_hbm,
+        vout_ref,
+        *refs,
+    ) = refs
+    *refs, vin_ref = refs
+    if inside:
+        final_hbm, *refs = refs
+        *refs, stage, f_sem, vsend, vrecv, y_buf, z_buf, y_s, y_r, z_s, z_r, v_s, v_r = refs
+    (
+        grads_ref,
+        wqkv,
+        wout,
+        wup,
+        wdown,
+        xr,
+        q_all,
+        k_all,
+        v_all,
+        prob,
+        att,
+        hr,
+        act,
+        slope,
+        n_one,
+        r_one,
+        n_two,
+        r_two,
+        gf,
+        ga,
+        go,
+        gq,
+        gk,
+        gv,
+        gqkv,
+        cur,
+        mid,
+        d0s,
+        d0r,
+        d1s,
+        d1r,
+        xsd,
+        xrv,
+        keep,
+        w_sem,
+        agx_s,
+        agx_r,
+        ags_s,
+        ags_r,
+        agf_s,
+        agf_r,
+        d0_s,
+        d0_r,
+        d1_s,
+        d1_r,
+        x_s,
+        x_r,
+    ) = refs
+    layers = obias_ref.shape[0]
+    shard, width = tokens_hbm.shape
     chunk = shard // CHUNKS
     heads_width = att.shape[2]
     window = LONGEST * SPAN
@@ -111,9 +124,17 @@
     cross = (1 - row) * 2 + col
     diag = (1 - row) * 2 + (1 - col)
 
+    own = pl.ds(pl.multiple_of(me * shard, shard), shard)
     loads = []
     for place, (src, dst) in enumerate(
-        ((wqkv_hbm, wqkv), (wout_hbm, wout), (wup_hbm, wup), (wdown_hbm, wdown))
+        (
+            (tokens_hbm, xr.at[0, own]),
+            (wqkv_hbm, wqkv),
+            (wout_hbm, wout),
+            (wup_hbm, wup),
+            (wdown_hbm, wdown),
+            (cot_hbm, gf.at[own]),
+        )
     ):
         load = pltpu.make_async_copy(src, dst, w_sem.at[place])
         load.start()
@@ -122,7 +143,16 @@
     barrier = pltpu.get_barrier_semaphore()
     for peer in (sib, cross):
         pl.semaphore_signal(barrier, inc=1, device_id={"tensor": peer}, device_id_type=MESH)
-    pl.semaphore_wait(barrier, 2)
+    if inside:
+        share = lax.axis_index("dp")
+        far, near = share // NEAR, share % NEAR
+        across = far * NEAR + (1 - near)
+        distant = [((far + hop) % FAR_SIDE) * NEAR + near for hop in range(1, FAR_SIDE)]
+        for peer in (across, *distant):
+            pl.semaphore_signal(barrier, inc=1, device_id={"dp": peer}, device_id_type=MESH)
+        pl.semaphore_wait(barrier, 3 + len(distant))
+    else:
+        pl.semaphore_wait(barrier, 2)
 
     def at_rows(owner, piece):
         return pl.ds(pl.multiple_of(owner * shard + piece * chunk, chunk), chunk)
@@ -133,13 +163,13 @@
     def part(piece):
         return pl.ds(piece * chunk, chunk)
 
-    def remote(src, dst, send, recv, peer):
+    def remote(src, dst, send, recv, peer, axis="tensor"):
         return pltpu.make_async_remote_copy(
             src_ref=src,
             dst_ref=dst,
             send_sem=send,
             recv_sem=recv,
-            device_id={"tensor": peer},
+            device_id={axis: peer},
             device_id_type=MESH,
         )
 
@@ -216,12 +246,12 @@
         centered = value - jnp.mean(value, axis=-1, keepdims=True)
         scale = lax.rsqrt(jnp.mean(centered * centered, axis=-1, keepdims=True) + EPSILON)
         unit = centered * scale
-        normed[layer, part(piece), :] = unit
+        normed[layer, part(piece), :] = unit.astype(BF16)
         inverse[layer, part(piece), :] = scale
         return unit * vec(layer, gain) + vec(layer, shift)
 
     def norm_backward(layer, piece, grad, gain, normed, inverse, rows):
-        unit = normed[layer, part(piece), :]
+        unit = normed[layer, part(piece), :].astype(F32)
         scale = inverse[layer, part(piece), :]
         scaled = grad * vec(layer, gain)
         out = scale * (
@@ -257,7 +287,7 @@
         limit = jnp.where(picture, span * SPAN + SPAN - 1, query_pos)
         key_pos = (span // LONGEST) * SPAN + lax.broadcasted_iota(jnp.int32, (1, window), 1)
         first = jnp.full((1, window), doc_ref[span] * SPAN, jnp.int32)
-        key_pos = jnp.where(key_pos >= first, key_pos, FAR)
+        key_pos = jnp.where(key_pos >= first, key_pos, BEYOND)
         allowed = key_pos <= limit
         for begin, wide, heads in groups:
             cols = pl.ds(begin, wide)
@@ -299,18 +329,19 @@
                 value_total = value_total + dot_tn(share, go_head)
             gk[keys, cols] = key_total
             gv[keys, cols] = value_total
-            gq[rows, cols] = total * 0.125
+            gq[rows, cols] = (total * 0.125).astype(BF16)
 
     def project(layer, owner):
         rows = span_rows(owner)
         out = dot_nn(xr[layer, rows, :], wqkv[layer])
-        bias = vec(layer, 7)
+        query_bias = vin_ref[layer, pl.ds(7, 1), pl.ds(0, heads_width)]
+        value_bias = vin_ref[layer, pl.ds(7, 1), pl.ds(256, heads_width)]
         q_all[layer, rows, :] = (
-            (out[:, :heads_width] + bias[:, :heads_width]) * 0.125
+            (out[:, :heads_width] + query_bias) * 0.125
         ).astype(BF16)
         k_all[layer, rows, :] = out[:, heads_width : 2 * heads_width].astype(BF16)
         v_all[layer, rows, :] = (
-            out[:, 2 * heads_width :] + bias[:, heads_width : 2 * heads_width]
+            out[:, 2 * heads_width :] + value_bias
         ).astype(BF16)
 
     def two(buf, first, second, piece):
@@ -361,18 +392,121 @@
 
         lax.fori_loop(0, width // 256, block, 0)
 
+    each = width // (NEAR * FAR_SIDE)
+    blocks = ((0, hidden), (hidden, hidden), (2 * hidden, 4 * heads_width))
+
+    def slice_rows(owner):
+        return pl.ds(pl.multiple_of(owner * each, each), each)
+
+    def near_copy(layer, block, place):
+        begin, wide = blocks[block]
+        return remote(
+            grads_ref.at[layer, slice_rows(place * NEAR + 1 - near), pl.ds(begin, wide)],
+            y_buf.at[layer, place, :, pl.ds(begin, wide)],
+            y_s.at[layer, block, place],
+            y_r.at[layer, block, place],
+            across,
+            "dp",
+        )
+
+    def far_copy(layer, block, hop):
+        begin, wide = blocks[block]
+        return remote(
+            grads_ref.at[layer, slice_rows(distant[hop]), pl.ds(begin, wide)],
+            z_buf.at[layer, hop, :, pl.ds(begin, wide)],
+            z_s.at[layer, block, hop],
+            z_r.at[layer, block, hop],
+            distant[hop],
+            "dp",
+        )
+
+    def near_send(layer, block):
+        if inside:
+            for hop in NEAR_ORDER:
+                near_copy(layer, block, far if hop is None else distant[hop] // NEAR).start()
+
+    def near_part(layer, block, hop):
+        begin, wide = blocks[block]
+        cols = pl.ds(begin, wide)
+        place = far if hop is None else distant[hop] // NEAR
+        near_copy(layer, block, place).wait_recv()
+        rows = slice_rows(place * NEAR + near)
+        grads_ref[layer, rows, cols] = (
+            grads_ref[layer, rows, cols].astype(F32) + y_buf[layer, place, :, cols].astype(F32)
+        ).astype(BF16)
+        if hop is not None:
+            far_copy(layer, block, hop).start()
+
+    def near_add(layer, block):
+        if inside:
+            for hop in NEAR_ORDER:
+                near_part(layer, block, hop)
+
+    staged = []
+
+    def far_add(layer, block):
+        begin, wide = blocks[block]
+        cols = pl.ds(begin, wide)
+        total = grads_ref[layer, slice_rows(share), cols].astype(F32)
+        for hop in range(FAR_SIDE - 1):
+            far_copy(layer, block, hop).wait_recv()
+            total = total + z_buf[layer, hop, :, cols].astype(F32)
+        slot = len(staged) % 2
+        if len(staged) > 1:
+            staged[-2].wait()
+        stage[slot] = total
+        staged.append(
+            pltpu.make_async_copy(stage.at[slot], final_hbm.at[layer, :, cols], f_sem.at[slot])
+        )
+        staged[-1].start()
+        for place in range(FAR_SIDE):
+            near_copy(layer, block, place).wait_send()
+        for hop in range(FAR_SIDE - 1):
+            far_copy(layer, block, hop).wait_send()
+
+    def vec_send(place, peers, axis):
+        vsend[place] = vout_ref[...]
+        copies = []
+        for order, peer in enumerate(peers):
+            slot = place + order
+            copies.append(
+                remote(vsend.at[place], vrecv.at[slot], v_s.at[slot], v_r.at[slot], peer, axis)
+            )
+        for copy in copies:
+            copy.start()
+        return copies, place
+
+    def vec_add(pending, whole):
+        copies, place = pending
+        for order, copy in enumerate(copies):
+            copy.wait_recv()
+            term = vrecv[place + order]
+            if not whole:
+                line = lax.broadcasted_iota(jnp.int32, term.shape, 1)
+                term = jnp.where(line < 6, term, 0.0)
+            vout_ref[...] += term
+        for copy in copies:
+            copy.wait_send()
+
+    for layer in range(layers):
+        vin_ref[layer, 0:4, :] = obias_ref[layer].astype(F32)
+        vin_ref[layer, 4:6, :] = gain_ref[layer].astype(F32)
+        vin_ref[layer, 6:7, :] = ubias_ref[layer : layer + 1, :].astype(F32)
+        for place in range(2):
+            vin_ref[layer, 7:8, place * 256 : place * 256 + heads_width] = hbias_ref[
+                layer, place : place + 1, :
+            ].astype(F32)
     vout_ref[...] = jnp.zeros_like(vout_ref)
-    cur[...] = tokens_ref[...].astype(F32)
+    loads[0].wait()
+    for piece in range(CHUNKS):
+        ag_send(FWD_ATTN, 0, piece, xr.at[0])
+    cur[...] = xr[0, own, :].astype(F32)
 
     def forward(layer, carry):
         here = xr.at[layer]
-        for piece in range(CHUNKS):
-            xr[layer, at_rows(me, piece), :] = cur[part(piece), :].astype(BF16)
-            ag_send(FWD_ATTN, layer, piece, here)
 
         @pl.when(layer == 0)
         def _():
-            loads[0].wait()
             loads[1].wait()
 
         project(layer, me)
@@ -382,8 +516,8 @@
 
         @pl.when(layer == 0)
         def _():
-            loads[2].wait()
-            loads[3].wait()
+            for load in loads[2:]:
+                load.wait()
 
         for piece in range(CHUNKS):
             ag_forward(FWD_ATTN, layer, piece, here)
@@ -411,13 +545,22 @@
         ffn_phase(FWD_FFN, layer, there, ffn_rows)
         for piece in range(CHUNKS):
             value = mid[part(piece), :] + rs_final(FWD_FFN, layer, piece) + vec(layer, 2)
-            cur[part(piece), :] = norm_forward(layer, piece, value, 5, 3, n_two, r_two)
+            value = norm_forward(layer, piece, value, 5, 3, n_two, r_two)
+            cur[part(piece), :] = value
+
+            @pl.when(layer + 1 < layers)
+            def _():
+                xr[layer + 1, at_rows(me, piece), :] = value.astype(BF16)
+                ag_send(FWD_ATTN, layer + 1, piece, xr.at[layer + 1])
+
         return carry
 
     lax.fori_loop(0, layers, forward, 0)
-    result_ref[...] = cur[...]
-
-    cur[...] = cot_ref[...].astype(F32)
+    store = pltpu.make_async_copy(cur, result_hbm, w_sem.at[6])
+    store.start()
+    store.wait()
+
+    cur[...] = gf[own, :].astype(F32)
 
     def backward(step, carry):
         layer = layers - 1 - step
@@ -426,8 +569,14 @@
             mid[part(piece), :] = grad
             gf[at_rows(me, piece), :] = grad.astype(BF16)
             ag_send(BWD_FFN, layer, piece, gf)
+
+        @pl.when(step > 0)
+        def _():
+            near_add(layer + 1, 2)
+
         ffn_phase(BWD_FFN, layer, gf, ffn_back_rows)
         weight_grad(layer, gf, act.at[layer], hidden, hidden)
+        near_send(layer, 1)
         for piece in range(CHUNKS):
             grad = mid[part(piece), :] + rs_final(BWD_FFN, layer, piece)
             grad = norm_backward(layer, piece, grad, 4, n_one, r_one, (4, 1, 0))
@@ -435,6 +584,7 @@
             ga[at_rows(me, piece), :] = grad.astype(BF16)
             ag_send(BWD_ATTN, layer, piece, ga)
         weight_grad(layer, hr.at[layer], slope.at[layer], 0, hidden)
+        near_send(layer, 0)
         vout_ref[layer, pl.ds(6, 1), :] = jnp.sum(
             slope[layer].astype(F32), axis=0, keepdims=True
         )
@@ -450,6 +600,7 @@
         for piece in range(CHUNKS):
             ag_recv("s", BWD_ATTN, layer, piece, ga).wait_recv()
         heads_grad(sib)
+        near_add(layer, 1)
         for piece in range(CHUNKS):
             ag_forward(BWD_ATTN, layer, piece, ga)
         heads_grad(cross)
@@ -458,7 +609,9 @@
         heads_grad(diag)
         for owner, send in ((diag, rs_diag), (cross, rs_cross), (sib, rs_sib), (me, None)):
             rows = span_rows(owner)
-            joined = jnp.concatenate((gq[rows, :], gk[rows, :], gv[rows, :]), axis=1).astype(BF16)
+            joined = jnp.concatenate(
+                (gq[rows, :], gk[rows, :].astype(BF16), gv[rows, :].astype(BF16)), axis=1
+            )
             gqkv[rows, :] = joined
             out = dot_nt(joined, wqkv[layer])
             for piece in range(CHUNKS):
@@ -470,15 +623,99 @@
         ag_done(BWD_ATTN, layer, ga)
         weight_grad(layer, xr.at[layer], gqkv, 2 * hidden, 3 * heads_width)
         weight_grad(layer, ga, att.at[layer], 2 * hidden + 3 * heads_width, heads_width)
+        near_send(layer, 2)
+        near_add(layer, 0)
         sums = jnp.sum(gqkv[...].astype(F32), axis=0, keepdims=True)
         vout_ref[layer, pl.ds(7, 1), pl.ds(0, heads_width)] = sums[:, :heads_width]
-        vout_ref[layer, pl.ds(7, 1), pl.ds(heads_width, heads_width)] = sums[:, 2 * heads_width :]
+        vout_ref[layer, pl.ds(7, 1), pl.ds(256, heads_width)] = sums[:, 2 * heads_width :]
         for piece in range(CHUNKS):
             cur[part(piece), :] = cur[part(piece), :] + rs_final(BWD_ATTN, layer, piece)
         return carry
 
     lax.fori_loop(0, layers, backward, 0)
-    tgrad_ref[...] = cur[...]
+    store = pltpu.make_async_copy(cur, tgrad_hbm, w_sem.at[7])
+    store.start()
+    if inside:
+        pending = vec_send(0, (sib,), "tensor")
+        for layer in range(layers - 1, 0, -1):
+            far_add(layer, 1)
+            far_add(layer, 0)
+        near_part(0, 2, NEAR_ORDER[0])
+        vec_add(pending, False)
+        pending = vec_send(1, (cross,), "tensor")
+        for layer in range(layers - 1, 0, -1):
+            far_add(layer, 2)
+        near_part(0, 2, NEAR_ORDER[1])
+        vec_add(pending, False)
+        pending = vec_send(2, (across,), "dp")
+        near_part(0, 2, NEAR_ORDER[2])
+        vec_add(pending, True)
+        pending = vec_send(3, distant, "dp")
+        near_part(0, 2, NEAR_ORDER[3])
+        far_add(0, 1)
+        far_add(0, 0)
+        vec_add(pending, True)
+        far_add(0, 2)
+        for copy in staged[-2:]:
+            copy.wait()
+    store.wait()
+
+
+def finish_kernel(hidden, heads_width, result, tgrad, vout, main, *outs):
+    layers, each, _ = main.shape
+    fine = each // GROUP
+    head_each = heads_width // (NEAR * FAR_SIDE)
+    place, mine = lax.axis_index("dp"), lax.axis_index("tensor")
+    res_o, tg_o, qkv_o, head_o, out_o, up_o, ubias_o, down_o, obias_o, gain_o = outs
+    res_o[...] = result[...]
+    tg_o[...] = tgrad[...]
+
+    def shifted(value, begin):
+        return pltpu.roll(value, value.shape[1] - begin, 1)
+
+    for layer in range(layers):
+        up_o[layer] = main[layer, :, :hidden]
+        down_o[layer] = main[layer, :, hidden : 2 * hidden].T
+        qkv_o[layer] = main[layer, :, 2 * hidden : 2 * hidden + 3 * heads_width]
+        out_o[layer] = main[layer, :, 2 * hidden + 3 * heads_width :].T
+        whole = vout[layer]
+        picked = shifted(whole, place * each + mine * fine)
+        obias_o[layer] = picked[0:4, :fine]
+        gain_o[layer] = picked[4:6, :fine]
+        ubias_o[layer : layer + 1, :] = shifted(whole, place * each)[6:7, :each]
+        picked = shifted(whole, place * head_each)
+        head_o[layer, 0:1, :] = picked[7:8, :head_each]
+        head_o[layer, 1:2, :] = picked[7:8, 256 : 256 + head_each]
+
+
+def finish(result, tokens_grad, vout, main, hidden, heads_width):
+    layers, each, _ = main.shape
+    fine = each // GROUP
+    head_each = heads_width // (NEAR * FAR_SIDE)
+    shapes = (
+        result.shape,
+        tokens_grad.shape,
+        (layers, each, 3 * heads_width),
+        (layers, 2, head_each),
+        (layers, heads_width, each),
+        (layers, each, hidden),
+        (layers, each),
+        (layers, hidden, each),
+        (layers, 4, fine),
+        (layers, 2, fine),
+    )
+    outs = pl.pallas_call(
+        partial(finish_kernel, hidden, heads_width),
+        name="finish",
+        out_shape=tuple(jax.ShapeDtypeStruct(shape, F32) for shape in shapes),
+        in_specs=[pl.BlockSpec(memory_space=pltpu.VMEM)] * 4,
+        out_specs=tuple(pl.BlockSpec(memory_space=pltpu.VMEM) for _ in shapes),
+    )(result, tokens_grad, vout, main)
+    return (
+        *outs[:2],
+        outs[2].reshape(layers, each, 3, heads_width),
+        *outs[3:],
+    )
 
 
 def body(
@@ -504,34 +741,47 @@
     total_width = 4 * heads_width + 2 * hidden
     chunk = shard // CHUNKS
     wide = max(hidden, width)
-    vin = jnp.concatenate(
-        (
-            out_bias,
-            norm_gain,
-            up_bias[:, None, :],
-            jnp.pad(
-                qv_bias.reshape(layers, 1, 2 * heads_width),
-                ((0, 0), (0, 0), (0, wide - 2 * heads_width)),
-            ),
-        ),
-        axis=1,
-    ).astype(F32)
     vmem = partial(pl.BlockSpec, memory_space=pltpu.VMEM)
     smem = partial(pl.BlockSpec, memory_space=pltpu.SMEM)
     anywhere = partial(pl.BlockSpec, memory_space=pl.ANY)
     sems = pltpu.SemaphoreType.DMA((4, layers, CHUNKS))
+    shares = lax.axis_size("dp")
+    inside = shares == NEAR * FAR_SIDE
+    rows_each = width // shares
+    outputs = [
+        jax.ShapeDtypeStruct((shard, width), F32),
+        jax.ShapeDtypeStruct((shard, width), F32),
+        jax.ShapeDtypeStruct((layers, 8, wide), F32),
+    ]
+    dma = pltpu.SemaphoreType.DMA
+    first, last = [], []
+    if inside:
+        outputs.append(jax.ShapeDtypeStruct((layers, rows_each, total_width), F32))
+        first = [pltpu.VMEM((layers, width, total_width), BF16)]
+        last = [
+            pltpu.VMEM((2, rows_each, hidden), F32),
+            dma((2,)),
+            pltpu.VMEM((4, layers, 8, wide), F32),
+            pltpu.VMEM((2 + FAR_SIDE, layers, 8, wide), F32),
+            pltpu.VMEM((layers, FAR_SIDE, rows_each, total_width), BF16),
+            pltpu.VMEM((layers, FAR_SIDE - 1, rows_each, total_width), BF16),
+            dma((layers, 3, FAR_SIDE)),
+            dma((layers, 3, FAR_SIDE)),
+            dma((layers, 3, FAR_SIDE - 1)),
+            dma((layers, 3, FAR_SIDE - 1)),
+            dma((2 + FAR_SIDE,)),
+            dma((2 + FAR_SIDE,)),
+        ]
+    else:
+        outputs.append(jax.ShapeDtypeStruct((layers, width, total_width), BF16))
     result, tokens_grad, vout, grads = pl.pallas_call(
-        step_kernel,
+        partial(step_kernel, inside),
         name="encoder_step",
-        out_shape=(
-            jax.ShapeDtypeStruct((shard, width), F32),
-            jax.ShapeDtypeStruct((shard, width), F32),
-            jax.ShapeDtypeStruct((layers, 8, wide), F32),
-            jax.ShapeDtypeStruct((layers, width, total_width), BF16),
-        ),
-        in_specs=[vmem(), vmem(), vmem(), smem(), smem()] + [anywhere()] * 4,
-        out_specs=(vmem(), vmem(), vmem(), vmem()),
-        scratch_shapes=[
+        out_shape=tuple(outputs),
+        in_specs=[anywhere()] * 2 + [vmem()] * 4 + [smem()] * 2 + [anywhere()] * 4,
+        out_specs=(anywhere(), anywhere(), vmem(), anywhere() if inside else vmem()),
+        scratch_shapes=first
+        + [
             pltpu.VMEM((layers, width, 3 * heads_width), BF16),
             pltpu.VMEM(out_weight.shape, BF16),
             pltpu.VMEM(up_weight.shape, BF16),
@@ -545,14 +795,14 @@
             pltpu.VMEM((layers, seq, width), BF16),
             pltpu.VMEM((layers, seq, hidden), BF16),
             pltpu.VMEM((layers, seq, hidden), BF16),
-            pltpu.VMEM((layers, shard, width), F32),
+            pltpu.VMEM((layers, shard, width), BF16),
             pltpu.VMEM((layers, shard, 1), F32),
-            pltpu.VMEM((layers, shard, width), F32),
+            pltpu.VMEM((layers, shard, width), BF16),
             pltpu.VMEM((layers, shard, 1), F32),
             pltpu.VMEM((seq, width), BF16),
             pltpu.VMEM((seq, width), BF16),
             pltpu.VMEM((seq, heads_width), BF16),
-            pltpu.VMEM((seq, heads_width), F32),
+            pltpu.VMEM((seq, heads_width), BF16),
             pltpu.VMEM((seq, heads_width), F32),
             pltpu.VMEM((seq, heads_width), F32),
             pltpu.VMEM((seq, 3 * heads_width), BF16),
@@ -560,15 +810,20 @@
             pltpu.VMEM((shard, width), F32),
         ]
         + [pltpu.VMEM((CHUNKS, chunk, width), BF16)] * 6
-        + [pltpu.VMEM((CHUNKS, chunk, width), F32), pltpu.SemaphoreType.DMA((4,))]
-        + [sems] * 12,
+        + [pltpu.VMEM((CHUNKS, chunk, width), F32), pltpu.SemaphoreType.DMA((8,))]
+        + [sems] * 12
+        + last
+        + [pltpu.VMEM((layers, 8, wide), F32)],
         compiler_params=pltpu.CompilerParams(
             collective_id=0, has_side_effects=True, vmem_limit_bytes=67043328
         ),
     )(
         tokens,
         cotangent,
-        vin,
+        out_bias,
+        norm_gain,
+        up_bias,
+        qv_bias,
         doc_start,
         picture,
         qkv_weight.reshape(layers, width, 3 * heads_width),
@@ -576,29 +831,33 @@
         up_weight,
         down_weight,
     )
-    shares = lax.axis_size("dp")
-    rows_each = width // shares
     head_each = heads_width // shares
     up_each = hidden // shares
     place = lax.axis_index("dp")
-    summed = [
-        lax.psum_scatter(grads[layer], "dp", scatter_dimension=0, tiled=True).astype(F32)
-        for layer in range(layers)
-    ]
-    main = jnp.stack(summed)
+    if inside:
+        return finish(result, tokens_grad, vout, grads, hidden, heads_width)
+    else:
+        main = jnp.stack(
+            [
+                lax.psum_scatter(grads[layer], "dp", scatter_dimension=0, tiled=True).astype(F32)
+                for layer in range(layers)
+            ]
+        )
+        vector_sum = lax.psum(vout[:, :6], ("dp", "tensor"))
+        bias_sum = lax.psum(vout[:, 6:], "dp")
     qkv_part = main[:, :, 2 * hidden : 2 * hidden + 3 * heads_width].reshape(
         layers, rows_each, 3, heads_width
     )
     out_part = main[:, :, 2 * hidden + 3 * heads_width :].transpose(0, 2, 1)
     up_part = main[:, :, :hidden]
     down_part = main[:, :, hidden : 2 * hidden].transpose(0, 2, 1)
-    vector_sum = lax.psum(vout[:, :6], ("dp", "tensor"))
-    bias_sum = lax.psum(vout[:, 6:], "dp")
     fine = width // (shares * GROUP)
     vector_sum = lax.dynamic_slice_in_dim(
         vector_sum, place * rows_each + lax.axis_index("tensor") * fine, fine, 2
     )
-    head_sum = bias_sum[:, 1, : 2 * heads_width].reshape(layers, 2, heads_width)
+    head_sum = jnp.stack(
+        (bias_sum[:, 1, :heads_width], bias_sum[:, 1, 256 : 256 + heads_width]), axis=1
+    )
     return (
         result,
         tokens_grad,

time: 384 us -> 234 us (0.61)
  waiting for transfers between devices: 84.1 us -> 0 us
  blocking collectives: 76.2 us -> 0 us
  Pallas kernels: 187 us -> 225 us
  between operations: 14.1 us -> 0.67 us
  local copies, waits for them, and re-layouts: 19.7 us -> 7.41 us
    reduce_scatter x2 -> x0, waiting for transfers between devices: 83.4 us -> none  [body(): lax.psum_scatter(grads[layer], 'dp', scatter_dimension=0, tiled=True)]
    psum x2 -> x0, blocking collectives: 76.2 us -> none  [the longest x1 38.3 us: body(): bias_sum = lax.psum(vout[:, 6:], 'dp')]
    pallas_call x1 -> x2, Pallas kernels: 187 us -> 225 us  [the longest x1 221 us: body(): pl.pallas_call(partial(step_kernel, inside), name='encoder_step', out_sha...]
    squeeze x1 -> x0, local copies, waits for them, and re-layouts: 6.48 us -> none  [body(): grads[layer]]
  transfers between devices with their start and end apart: 2 -> 0, of which waited for: 2 -> 0; matrix products, arithmetic and copies ran while one was open for 1% -> 0% of each run, Pallas kernels for 0% -> 0%
where the time goes in v3:
time: 234 us; the launch traced here: 233 us
  Pallas kernels  225 us (96%)
  local copies, waits for them, and re-layouts  7.41 us (3%)
    pallas_call x1, Pallas kernels, body(): pl.pallas_call(partial(step_kernel, inside), name='encoder_step', out_sha...  221 us

profile of v3, /device:TPU:0, one launch (start us, length us, event | category | flops | bytes accessed | tf_op | source)
XLA Modules:
  0.0 233.3 jit_solution(4485576741336776950)
XLA Ops:
  0.6 3.9 %copy.25.refs_8_ = bf16[2,768,576]{2,1,0:T(8,128)(2,1)} copy(bf16[2,768,576]{1,2,0:T(8,128)(2,1)} %bitcast.3) | data formatting | bytes 3538944 | tf_op jit(solution)/shard_map/reshape | solution.py:829
  4.6 221.0 %encoder_step.1 = (f32[256,768]{1,0:T(8,128)}, f32[256,768]{1,0:T(8,128)}, f32[2,8,768]{2,1,0:T(8,128)}, f32[2,96,2304]{2,1,0:T(8,128)}) custom-call(bf16[256,768]{1,0:T(8,128)(2,1)} %refs_0_.1, bf16[256,768]{1,0:T(8,128)(2,1)} %refs_1_.1, bf16[2,4,768]{2,1,0:T(4,128)(2,1)} %refs_2_.1, bf16[2,2,768]{2,1,0:T(2,128)(2,1)} %refs_3_.1, bf16[2,768]{1,0:T(2,128)(2,1)} %refs_4_.1, ...), custom_call_target="tpu_custom_call" | custom-call | tf_op jit(solution)/shard_map/encoder_step/pallas_call | solution.py:777
  225.5 4.2 %finish.1 = (f32[256,768]{1,0:T(8,128)}, f32[256,768]{1,0:T(8,128)}, f32[2,96,576]{2,1,0:T(8,128)}, f32[2,2,24]{2,1,0:T(2,128)}, f32[2,192,96]{2,1,0:T(8,128)}, ...) custom-call(f32[256,768]{1,0:T(8,128)} %get-tuple-element.24.result,, ...), custom_call_target="tpu_custom_call" | custom-call | tf_op jit(solution)/shard_map/finish/pallas_call | solution.py:707
  229.8 0.0 copy-start
  229.8 1.3 copy.26
  231.1 1.1 copy.27
  232.2 0.0 copy-done
  232.2 1.1 copy.28
Async XLA Ops:
  229.8 2.4 %copy-start = (f32[2,768,96]{2,1,0:T(8,128)S(1)}, f32[2,768,96]{2,1,0:T(8,128)}, u32[]{:S(2)}) copy-start(f32[2,768,96]{2,1,0:T(8,128)} %get-tuple-element.55) | copy-start | bytes 1769476

commit v4 on v3

--- a/solution.py
+++ b/solution.py
@@ -12,10 +12,13 @@
 GROUP = 4
 LONGEST = 3
 CHUNKS = 2
+HALVES = 2
 EPSILON = 1e-05
 BEYOND = 1 << 20
 NEAR, FAR_SIDE = 2, 4
 NEAR_ORDER = (1, 0, 2, None)
+OUT_WIDE, QKV_WIDE = 256, 640
+UP, DOWN, OUT, QKV = range(4)
 F32 = jnp.float32
 BF16 = jnp.bfloat16
 MESH = pl.DeviceIdType.MESH
@@ -115,8 +118,8 @@
     layers = obias_ref.shape[0]
     shard, width = tokens_hbm.shape
     chunk = shard // CHUNKS
+    part_rows = shard // HALVES
     heads_width = att.shape[2]
-    window = LONGEST * SPAN
     hidden = wup.shape[2]
     me = lax.axis_index("tensor")
     row, col = me // 2, me % 2
@@ -157,6 +160,9 @@
     def at_rows(owner, piece):
         return pl.ds(pl.multiple_of(owner * shard + piece * chunk, chunk), chunk)
 
+    def half_rows(owner, half):
+        return pl.ds(pl.multiple_of(owner * shard + half * part_rows, part_rows), part_rows)
+
     def span_rows(owner):
         return pl.ds(pl.multiple_of(owner * shard, shard), shard)
 
@@ -231,6 +237,23 @@
         d1s[piece] = value.astype(BF16)
         rs_copy("d1", phase, layer, piece).start()
 
+    def place_part(phase, layer, pair, which, piece, value):
+        @pl.when((pair == 0) & (which == 0))
+        def _():
+            rs_diag(phase, layer, piece, value)
+
+        @pl.when((pair == 0) & (which == 1))
+        def _():
+            rs_cross(phase, layer, piece, value)
+
+        @pl.when((pair == 1) & (which == 0))
+        def _():
+            rs_sib(phase, layer, piece, value)
+
+        @pl.when((pair == 1) & (which == 1))
+        def _():
+            keep[piece] = value
+
     def rs_final(phase, layer, piece):
         rs_copy("d1", phase, layer, piece).wait_recv()
         rs_copy("x", phase, layer, piece).wait_recv()
@@ -276,17 +299,30 @@
         low = head * HEAD_DIM - begin
         return jnp.where((lane >= low) & (lane < low + HEAD_DIM), value, jnp.zeros_like(value))
 
-    def window_of(span):
-        return pl.ds(pl.multiple_of((span // LONGEST) * SPAN, SPAN), window)
-
-    def attend(layer, span):
-        rows = span_rows(span)
-        keys = window_of(span)
-        query_pos = span * SPAN + lax.broadcasted_iota(jnp.int32, (SPAN, 1), 0)
-        picture = jnp.full((SPAN, 1), pic_ref[span], jnp.int32) == 1
+    def by_keys(span, run):
+        for count in range(1, LONGEST + 1):
+
+            @pl.when((span == count - 1) if count < LONGEST else (span >= count - 1))
+            def _():
+                run(count)
+
+    def keys_of(span, count):
+        if count < LONGEST:
+            return 0, pl.ds(0, count * SPAN), (count * (count - 1)) // 2
+        begin = span - (LONGEST - 1)
+        rows = pl.ds(pl.multiple_of(begin * SPAN, SPAN), LONGEST * SPAN)
+        return begin * SPAN, rows, LONGEST * (span - 1)
+
+    def attend(layer, span, half, count):
+        rows = half_rows(span, half)
+        first_key, keys, base = keys_of(span, count)
+        query_pos = (
+            span * SPAN + half * part_rows + lax.broadcasted_iota(jnp.int32, (part_rows, 1), 0)
+        )
+        picture = jnp.full((part_rows, 1), pic_ref[span], jnp.int32) == 1
         limit = jnp.where(picture, span * SPAN + SPAN - 1, query_pos)
-        key_pos = (span // LONGEST) * SPAN + lax.broadcasted_iota(jnp.int32, (1, window), 1)
-        first = jnp.full((1, window), doc_ref[span] * SPAN, jnp.int32)
+        key_pos = first_key + lax.broadcasted_iota(jnp.int32, (1, count * SPAN), 1)
+        first = jnp.full((1, count * SPAN), doc_ref[span] * SPAN, jnp.int32)
         key_pos = jnp.where(key_pos >= first, key_pos, BEYOND)
         allowed = key_pos <= limit
         for begin, wide, heads in groups:
@@ -294,20 +330,23 @@
             q_here = q_all[layer, rows, cols]
             k_here = k_all[layer, keys, cols]
             v_here = v_all[layer, keys, cols]
-            total = jnp.zeros((SPAN, wide), F32)
+            total = jnp.zeros((part_rows, wide), F32)
             for head in heads:
                 scores = dot_nt(only_head(q_here, begin, head), k_here)
                 scores = jnp.where(allowed, scores, -1e30)
                 raised = jnp.exp(scores - jnp.max(scores, axis=-1, keepdims=True))
                 share = raised * (1.0 / jnp.sum(raised, axis=-1, keepdims=True))
                 share = share.astype(BF16)
-                prob[layer, span, head] = share
+                for block in range(count):
+                    prob[layer, head, base + block, pl.ds(half * part_rows, part_rows), :] = share[
+                        :, block * SPAN : (block + 1) * SPAN
+                    ]
                 total = total + dot_nn(share, only_head(v_here, begin, head))
             att[layer, rows, cols] = total.astype(BF16)
 
-    def attend_back(layer, span):
+    def attend_back(layer, span, count):
         rows = span_rows(span)
-        keys = window_of(span)
+        _, keys, base = keys_of(span, count)
         for begin, wide, heads in groups:
             cols = pl.ds(begin, wide)
             q_here = q_all[layer, rows, cols]
@@ -322,7 +361,9 @@
                 go_head = only_head(go_here, begin, head)
                 inner = jnp.sum(only_head(mixed, begin, head), axis=-1, keepdims=True)
                 gp = dot_nt(go_head, v_here)
-                share = prob[layer, span, head]
+                share = jnp.concatenate(
+                    [prob[layer, head, base + block] for block in range(count)], axis=1
+                )
                 gs = (share.astype(F32) * (gp - inner)).astype(BF16)
                 total = total + dot_nn(gs, only_head(k_here, begin, head))
                 key_total = key_total + dot_tn(gs, only_head(q_here, begin, head))
@@ -331,9 +372,13 @@
             gv[keys, cols] = value_total
             gq[rows, cols] = (total * 0.125).astype(BF16)
 
+    def member(pair, which):
+        line = (1 - pair) * (1 - row) + pair * row
+        return line * 2 + (1 - which) * (1 - col) + which * col
+
     def project(layer, owner):
         rows = span_rows(owner)
-        out = dot_nn(xr[layer, rows, :], wqkv[layer])
+        out = dot_nt(xr[layer, rows, :], wqkv[layer])
         query_bias = vin_ref[layer, pl.ds(7, 1), pl.ds(0, heads_width)]
         value_bias = vin_ref[layer, pl.ds(7, 1), pl.ds(256, heads_width)]
         q_all[layer, rows, :] = (
@@ -393,7 +438,12 @@
         lax.fori_loop(0, width // 256, block, 0)
 
     each = width // (NEAR * FAR_SIDE)
-    blocks = ((0, hidden), (hidden, hidden), (2 * hidden, 4 * heads_width))
+    blocks = (
+        (0, hidden),
+        (hidden, hidden),
+        (2 * hidden, OUT_WIDE),
+        (2 * hidden + OUT_WIDE, QKV_WIDE),
+    )
 
     def slice_rows(owner):
         return pl.ds(pl.multiple_of(owner * each, each), each)
@@ -454,9 +504,11 @@
         slot = len(staged) % 2
         if len(staged) > 1:
             staged[-2].wait()
-        stage[slot] = total
+        stage[slot, :, pl.ds(0, wide)] = total
         staged.append(
-            pltpu.make_async_copy(stage.at[slot], final_hbm.at[layer, :, cols], f_sem.at[slot])
+            pltpu.make_async_copy(
+                stage.at[slot, :, pl.ds(0, wide)], final_hbm.at[layer, :, cols], f_sem.at[slot]
+            )
         )
         staged[-1].start()
         for place in range(FAR_SIDE):
@@ -464,17 +516,19 @@
         for hop in range(FAR_SIDE - 1):
             far_copy(layer, block, hop).wait_send()
 
-    def vec_send(place, peers, axis):
-        vsend[place] = vout_ref[...]
+    def vec_copies(place, peers, axis):
         copies = []
         for order, peer in enumerate(peers):
             slot = place + order
             copies.append(
                 remote(vsend.at[place], vrecv.at[slot], v_s.at[slot], v_r.at[slot], peer, axis)
             )
-        for copy in copies:
+        return copies, place
+
+    def vec_send(place, peers, axis):
+        vsend[place] = vout_ref[...]
+        for copy in vec_copies(place, peers, axis)[0]:
             copy.start()
-        return copies, place
 
     def vec_add(pending, whole):
         copies, place = pending
@@ -497,6 +551,12 @@
                 layer, place : place + 1, :
             ].astype(F32)
     vout_ref[...] = jnp.zeros_like(vout_ref)
+    for begin, wide, room in (
+        (2 * hidden, heads_width, OUT_WIDE),
+        (2 * hidden + OUT_WIDE, 3 * heads_width, QKV_WIDE),
+    ):
+        blank = (layers, width, room - wide)
+        grads_ref[:, :, begin + wide : begin + room] = jnp.zeros(blank, BF16)
     loads[0].wait()
     for piece in range(CHUNKS):
         ag_send(FWD_ATTN, 0, piece, xr.at[0])
@@ -525,15 +585,24 @@
         for piece in range(CHUNKS):
             ag_recv("f", FWD_ATTN, layer, piece, here).wait_recv()
         project(layer, diag)
-        for owner, send in ((diag, rs_diag), (cross, rs_cross), (sib, rs_sib), (me, None)):
-            attend(layer, owner)
-            out = dot_nn(att[layer, span_rows(owner), :], wout[layer])
-            for piece in range(CHUNKS):
-                value = out[piece * chunk : (piece + 1) * chunk]
-                if send is None:
-                    keep[piece] = value
-                else:
-                    send(FWD_ATTN, layer, piece, value)
+
+        def heads_out(turn, inner):
+            pair, half, which = turn // (2 * HALVES), (turn % (2 * HALVES)) // 2, turn % 2
+            owner = member(pair, which)
+            by_keys(owner, partial(attend, layer, owner, half))
+            out = dot_nn(att[layer, half_rows(owner, half), :], wout[layer])
+            for piece in range(CHUNKS // HALVES):
+                place_part(
+                    FWD_ATTN,
+                    layer,
+                    pair,
+                    which,
+                    half * (CHUNKS // HALVES) + piece,
+                    out[piece * chunk : (piece + 1) * chunk],
+                )
+            return inner
+
+        lax.fori_loop(0, 4 * HALVES, heads_out, 0)
         ag_done(FWD_ATTN, layer, here)
         there = hr.at[layer]
         for piece in range(CHUNKS):
@@ -570,13 +639,15 @@
             gf[at_rows(me, piece), :] = grad.astype(BF16)
             ag_send(BWD_FFN, layer, piece, gf)
 
+        ffn_phase(BWD_FFN, layer, gf, ffn_back_rows)
+        weight_grad(layer, gf, act.at[layer], hidden, hidden)
+        near_send(layer, DOWN)
+
         @pl.when(step > 0)
         def _():
-            near_add(layer + 1, 2)
-
-        ffn_phase(BWD_FFN, layer, gf, ffn_back_rows)
-        weight_grad(layer, gf, act.at[layer], hidden, hidden)
-        near_send(layer, 1)
+            near_add(layer + 1, OUT)
+            near_add(layer + 1, QKV)
+
         for piece in range(CHUNKS):
             grad = mid[part(piece), :] + rs_final(BWD_FFN, layer, piece)
             grad = norm_backward(layer, piece, grad, 4, n_one, r_one, (4, 1, 0))
@@ -584,78 +655,110 @@
             ga[at_rows(me, piece), :] = grad.astype(BF16)
             ag_send(BWD_ATTN, layer, piece, ga)
         weight_grad(layer, hr.at[layer], slope.at[layer], 0, hidden)
-        near_send(layer, 0)
+        near_send(layer, UP)
         vout_ref[layer, pl.ds(6, 1), :] = jnp.sum(
             slope[layer].astype(F32), axis=0, keepdims=True
         )
         gk[...] = jnp.zeros_like(gk)
         gv[...] = jnp.zeros_like(gv)
 
-        def heads_grad(owner):
+        def heads_grad(turn, inner):
+            @pl.when(turn == 1)
+            def _():
+                for piece in range(CHUNKS):
+                    ag_recv("s", BWD_ATTN, layer, piece, ga).wait_recv()
+
+            @pl.when(turn == 2)
+            def _():
+                for piece in range(CHUNKS):
+                    ag_forward(BWD_ATTN, layer, piece, ga)
+                    if piece == 0:
+                        near_add(layer, DOWN)
+
+            @pl.when(turn == 3)
+            def _():
+                for piece in range(CHUNKS):
+                    ag_recv("f", BWD_ATTN, layer, piece, ga).wait_recv()
+
+            owner = member(1 - turn // 2, 1 - turn % 2)
             rows = span_rows(owner)
             go[rows, :] = dot_nt(ga[rows, :], wout[layer]).astype(BF16)
-            attend_back(layer, owner)
-
-        heads_grad(me)
-        for piece in range(CHUNKS):
-            ag_recv("s", BWD_ATTN, layer, piece, ga).wait_recv()
-        heads_grad(sib)
-        near_add(layer, 1)
-        for piece in range(CHUNKS):
-            ag_forward(BWD_ATTN, layer, piece, ga)
-        heads_grad(cross)
-        for piece in range(CHUNKS):
-            ag_recv("f", BWD_ATTN, layer, piece, ga).wait_recv()
-        heads_grad(diag)
-        for owner, send in ((diag, rs_diag), (cross, rs_cross), (sib, rs_sib), (me, None)):
-            rows = span_rows(owner)
+            by_keys(owner, partial(attend_back, layer, owner))
+            return inner
+
+        lax.fori_loop(0, GROUP, heads_grad, 0)
+
+        def rows_back(turn, inner):
+            @pl.when(turn == 2)
+            def _():
+                weight_grad(layer, ga, att.at[layer], 2 * hidden, heads_width)
+                near_send(layer, OUT)
+
+            pair, which = turn // 2, turn % 2
+            rows = span_rows(member(pair, which))
             joined = jnp.concatenate(
                 (gq[rows, :], gk[rows, :].astype(BF16), gv[rows, :].astype(BF16)), axis=1
             )
             gqkv[rows, :] = joined
-            out = dot_nt(joined, wqkv[layer])
+            out = dot_nn(joined, wqkv[layer])
             for piece in range(CHUNKS):
-                value = out[piece * chunk : (piece + 1) * chunk]
-                if send is None:
-                    keep[piece] = value
-                else:
-                    send(BWD_ATTN, layer, piece, value)
+                place_part(
+                    BWD_ATTN, layer, pair, which, piece, out[piece * chunk : (piece + 1) * chunk]
+                )
+            return inner
+
+        lax.fori_loop(0, GROUP, rows_back, 0)
         ag_done(BWD_ATTN, layer, ga)
-        weight_grad(layer, xr.at[layer], gqkv, 2 * hidden, 3 * heads_width)
-        weight_grad(layer, ga, att.at[layer], 2 * hidden + 3 * heads_width, heads_width)
-        near_send(layer, 2)
-        near_add(layer, 0)
+        weight_grad(layer, xr.at[layer], gqkv, 2 * hidden + OUT_WIDE, 3 * heads_width)
+        near_send(layer, QKV)
         sums = jnp.sum(gqkv[...].astype(F32), axis=0, keepdims=True)
         vout_ref[layer, pl.ds(7, 1), pl.ds(0, heads_width)] = sums[:, :heads_width]
         vout_ref[layer, pl.ds(7, 1), pl.ds(256, heads_width)] = sums[:, 2 * heads_width :]
+        if inside:
+
+            @pl.when(step == layers - 1)
+            def _():
+                vec_send(0, (sib,), "tensor")
+                near_add(layer, UP)
+                vec_add(vec_copies(0, (sib,), "tensor"), False)
+                vec_send(1, (cross,), "tensor")
+                near_add(layer, OUT)
+
+            @pl.when(step < layers - 1)
+            def _():
+                near_add(layer, UP)
+
         for piece in range(CHUNKS):
             cur[part(piece), :] = cur[part(piece), :] + rs_final(BWD_ATTN, layer, piece)
+        if inside:
+
+            @pl.when(step == layers - 1)
+            def _():
+                vec_add(vec_copies(1, (cross,), "tensor"), False)
+                vec_send(2, (across,), "dp")
+
         return carry
 
     lax.fori_loop(0, layers, backward, 0)
     store = pltpu.make_async_copy(cur, tgrad_hbm, w_sem.at[7])
     store.start()
     if inside:
-        pending = vec_send(0, (sib,), "tensor")
-        for layer in range(layers - 1, 0, -1):
-            far_add(layer, 1)
-            far_add(layer, 0)
-        near_part(0, 2, NEAR_ORDER[0])
-        vec_add(pending, False)
-        pending = vec_send(1, (cross,), "tensor")
-        for layer in range(layers - 1, 0, -1):
-            far_add(layer, 2)
-        near_part(0, 2, NEAR_ORDER[1])
-        vec_add(pending, False)
-        pending = vec_send(2, (across,), "dp")
-        near_part(0, 2, NEAR_ORDER[2])
-        vec_add(pending, True)
-        pending = vec_send(3, distant, "dp")
-        near_part(0, 2, NEAR_ORDER[3])
-        far_add(0, 1)
-        far_add(0, 0)
-        vec_add(pending, True)
-        far_add(0, 2)
+        older = [
+            (layer, block)
+            for layer in range(layers - 1, 0, -1)
+            for block in (DOWN, UP, OUT, QKV)
+        ]
+        near_part(0, QKV, NEAR_ORDER[0])
+        vec_add(vec_copies(2, (across,), "dp"), True)
+        vec_send(3, distant, "dp")
+        for place, hop in enumerate(NEAR_ORDER[1:]):
+            for layer, block in older[place :: FAR_SIDE - 1]:
+                far_add(layer, block)
+            near_part(0, QKV, hop)
+        for block in (DOWN, UP, OUT):
+            far_add(0, block)
+        vec_add(vec_copies(3, distant, "dp"), True)
+        far_add(0, QKV)
         for copy in staged[-2:]:
             copy.wait()
     store.wait()
@@ -675,9 +778,13 @@
 
     for layer in range(layers):
         up_o[layer] = main[layer, :, :hidden]
-        down_o[layer] = main[layer, :, hidden : 2 * hidden].T
-        qkv_o[layer] = main[layer, :, 2 * hidden : 2 * hidden + 3 * heads_width]
-        out_o[layer] = main[layer, :, 2 * hidden + 3 * heads_width :].T
+        down_o[layer] = main[layer, :, hidden : 2 * hidden]
+        out_o[layer] = main[layer, :, 2 * hidden : 2 * hidden + heads_width].T
+        begin = 2 * hidden + OUT_WIDE
+        for third in range(3):
+            qkv_o[layer, third] = main[
+                layer, :, begin + third * heads_width : begin + (third + 1) * heads_width
+            ]
         whole = vout[layer]
         picked = shifted(whole, place * each + mine * fine)
         obias_o[layer] = picked[0:4, :fine]
@@ -695,12 +802,12 @@
     shapes = (
         result.shape,
         tokens_grad.shape,
-        (layers, each, 3 * heads_width),
+        (layers, 3, each, heads_width),
         (layers, 2, head_each),
         (layers, heads_width, each),
         (layers, each, hidden),
         (layers, each),
-        (layers, hidden, each),
+        (layers, each, hidden),
         (layers, 4, fine),
         (layers, 2, fine),
     )
@@ -713,8 +820,10 @@
     )(result, tokens_grad, vout, main)
     return (
         *outs[:2],
-        outs[2].reshape(layers, each, 3, heads_width),
-        *outs[3:],
+        outs[2].transpose(0, 2, 1, 3),
+        *outs[3:7],
+        outs[7].transpose(0, 2, 1),
+        *outs[8:],
     )
 
 
@@ -737,8 +846,9 @@
     seq = shard * GROUP
     hidden = up_weight.shape[2]
     spans = seq // SPAN
+    pairs = sum(min(span + 1, LONGEST) for span in range(spans))
     heads = heads_width // HEAD_DIM
-    total_width = 4 * heads_width + 2 * hidden
+    total_width = 2 * hidden + OUT_WIDE + QKV_WIDE
     chunk = shard // CHUNKS
     wide = max(hidden, width)
     vmem = partial(pl.BlockSpec, memory_space=pltpu.VMEM)
@@ -765,10 +875,10 @@
             pltpu.VMEM((2 + FAR_SIDE, layers, 8, wide), F32),
             pltpu.VMEM((layers, FAR_SIDE, rows_each, total_width), BF16),
             pltpu.VMEM((layers, FAR_SIDE - 1, rows_each, total_width), BF16),
-            dma((layers, 3, FAR_SIDE)),
-            dma((layers, 3, FAR_SIDE)),
-            dma((layers, 3, FAR_SIDE - 1)),
-            dma((layers, 3, FAR_SIDE - 1)),
+            dma((layers, 4, FAR_SIDE)),
+            dma((layers, 4, FAR_SIDE)),
+            dma((layers, 4, FAR_SIDE - 1)),
+            dma((layers, 4, FAR_SIDE - 1)),
             dma((2 + FAR_SIDE,)),
             dma((2 + FAR_SIDE,)),
         ]
@@ -782,7 +892,7 @@
         out_specs=(anywhere(), anywhere(), vmem(), anywhere() if inside else vmem()),
         scratch_shapes=first
         + [
-            pltpu.VMEM((layers, width, 3 * heads_width), BF16),
+            pltpu.VMEM((layers, 3 * heads_width, width), BF16),
             pltpu.VMEM(out_weight.shape, BF16),
             pltpu.VMEM(up_weight.shape, BF16),
             pltpu.VMEM(down_weight.shape, BF16),
@@ -790,7 +900,7 @@
             pltpu.VMEM((layers, seq, heads_width), BF16),
             pltpu.VMEM((layers, seq, heads_width), BF16),
             pltpu.VMEM((layers, seq, heads_width), BF16),
-            pltpu.VMEM((layers, spans, heads, SPAN, LONGEST * SPAN), BF16),
+            pltpu.VMEM((layers, heads, pairs, SPAN, SPAN), BF16),
             pltpu.VMEM((layers, seq, heads_width), BF16),
             pltpu.VMEM((layers, seq, width), BF16),
             pltpu.VMEM((layers, seq, hidden), BF16),
@@ -826,7 +936,7 @@
         qv_bias,
         doc_start,
         picture,
-        qkv_weight.reshape(layers, width, 3 * heads_width),
+        qkv_weight.transpose(0, 2, 3, 1).reshape(layers, 3 * heads_width, width),
         out_weight,
         up_weight,
         down_weight,
@@ -845,10 +955,11 @@
         )
         vector_sum = lax.psum(vout[:, :6], ("dp", "tensor"))
         bias_sum = lax.psum(vout[:, 6:], "dp")
-    qkv_part = main[:, :, 2 * hidden : 2 * hidden + 3 * heads_width].reshape(
+    begin = 2 * hidden + OUT_WIDE
+    qkv_part = main[:, :, begin : begin + 3 * heads_width].reshape(
         layers, rows_each, 3, heads_width
     )
-    out_part = main[:, :, 2 * hidden + 3 * heads_width :].transpose(0, 2, 1)
+    out_part = main[:, :, 2 * hidden : 2 * hidden + heads_width].transpose(0, 2, 1)
     up_part = main[:, :, :hidden]
     down_part = main[:, :, hidden : 2 * hidden].transpose(0, 2, 1)
     fine = width // (shares * GROUP)

time: 234 us -> 222 us (0.949)
  local copies, waits for them, and re-layouts: 7.41 us -> 0 us
  Pallas kernels: 225 us -> 221 us
    pallas_call x1, Pallas kernels: 221 us -> 217 us  [body(): pl.pallas_call(partial(step_kernel, inside), name='encoder_step', out_sha...]
    reshape x1 -> x0, local copies, waits for them, and re-layouts: 3.93 us -> none  [body(): qkv_weight.reshape(layers, width, 3 * heads_width)]
where the time goes in v4:
time: 222 us; the launch traced here: 221 us
  Pallas kernels  221 us (100%)
    pallas_call x1, Pallas kernels, body(): pl.pallas_call(partial(step_kernel, inside), name='encoder_step', out_sha...  217 us

profile of v4, /device:TPU:0, one launch (start us, length us, event | category | flops | bytes accessed | tf_op | source)
XLA Modules:
  0.0 221.5 jit_solution(10466931439408517414)
XLA Ops:
  0.6 216.6 %encoder_step.1 = (f32[256,768]{1,0:T(8,128)}, f32[256,768]{1,0:T(8,128)}, f32[2,8,768]{2,1,0:T(8,128)}, f32[2,96,2432]{2,1,0:T(8,128)}) custom-call(bf16[256,768]{1,0:T(8,128)(2,1)} %refs_0_.1, bf16[256,768]{1,0:T(8,128)(2,1)} %refs_1_.1, bf16[2,4,768]{2,1,0:T(4,128)(2,1)} %refs_2_.1, bf16[2,2,768]{2,1,0:T(2,128)(2,1)} %refs_3_.1, bf16[2,768]{1,0:T(2,128)(2,1)} %refs_4_.1, ...), custom_call_target="tpu_custom_call" | custom-call | tf_op jit(solution)/shard_map/encoder_step/pallas_call | solution.py:887
  217.3 4.0 %finish.1 = (f32[256,768]{1,0:T(8,128)}, f32[256,768]{1,0:T(8,128)}, f32[2,3,96,192]{3,2,1,0:T(8,128)}, f32[2,2,24]{2,1,0:T(2,128)}, f32[2,192,96]{2,1,0:T(8,128...) custom-call(f32[256,768]{1,0:T(8,128)} %get-tuple-element.24.result,, ...), custom_call_target="tpu_custom_call" | custom-call | tf_op jit(solution)/shard_map/finish/pallas_call | solution.py:814

commit v5 on v4

--- a/solution.py
+++ b/solution.py
@@ -287,6 +287,17 @@
             vout_ref[layer, pl.ds(place, 1), :] += jnp.sum(term, axis=0, keepdims=True)
         return out
 
+    def begin_back(layer, piece, grad):
+        grad = norm_backward(layer, piece, grad, 5, n_two, r_two, (5, 3, 2))
+        mid[part(piece), :] = grad
+        gf[at_rows(me, piece), :] = grad.astype(BF16)
+        ag_send(BWD_FFN, layer, piece, gf)
+
+    def result_copy(piece):
+        return pltpu.make_async_copy(
+            keep.at[piece], result_hbm.at[part(piece)], w_sem.at[6 + piece]
+        )
+
     groups = []
     for begin in range(0, heads_width, 128):
         wide = min(128, heads_width - begin)
@@ -526,7 +537,7 @@
         return copies, place
 
     def vec_send(place, peers, axis):
-        vsend[place] = vout_ref[...]
+        vsend[place] = vout_ref[...].astype(BF16)
         for copy in vec_copies(place, peers, axis)[0]:
             copy.start()
 
@@ -534,7 +545,7 @@
         copies, place = pending
         for order, copy in enumerate(copies):
             copy.wait_recv()
-            term = vrecv[place + order]
+            term = vrecv[place + order].astype(F32)
             if not whole:
                 line = lax.broadcasted_iota(jnp.int32, term.shape, 1)
                 term = jnp.where(line < 6, term, 0.0)
@@ -617,6 +628,12 @@
             value = norm_forward(layer, piece, value, 5, 3, n_two, r_two)
             cur[part(piece), :] = value
 
+            @pl.when(layer + 1 == layers)
+            def _():
+                keep[piece] = value
+                result_copy(piece).start()
+                begin_back(layer, piece, gf[at_rows(me, piece), :].astype(F32))
+
             @pl.when(layer + 1 < layers)
             def _():
                 xr[layer + 1, at_rows(me, piece), :] = value.astype(BF16)
@@ -625,19 +642,16 @@
         return carry
 
     lax.fori_loop(0, layers, forward, 0)
-    store = pltpu.make_async_copy(cur, result_hbm, w_sem.at[6])
-    store.start()
-    store.wait()
-
-    cur[...] = gf[own, :].astype(F32)
+
 
     def backward(step, carry):
         layer = layers - 1 - step
-        for piece in range(CHUNKS):
-            grad = norm_backward(layer, piece, cur[part(piece), :], 5, n_two, r_two, (5, 3, 2))
-            mid[part(piece), :] = grad
-            gf[at_rows(me, piece), :] = grad.astype(BF16)
-            ag_send(BWD_FFN, layer, piece, gf)
+
+        @pl.when(step == 0)
+        def _():
+            for piece in range(CHUNKS):
+                result_copy(piece).wait()
+
 
         ffn_phase(BWD_FFN, layer, gf, ffn_back_rows)
         weight_grad(layer, gf, act.at[layer], hidden, hidden)
@@ -645,7 +659,6 @@
 
         @pl.when(step > 0)
         def _():
-            near_add(layer + 1, OUT)
             near_add(layer + 1, QKV)
 
         for piece in range(CHUNKS):
@@ -727,9 +740,16 @@
             @pl.when(step < layers - 1)
             def _():
                 near_add(layer, UP)
+                near_add(layer, OUT)
 
         for piece in range(CHUNKS):
-            cur[part(piece), :] = cur[part(piece), :] + rs_final(BWD_ATTN, layer, piece)
+            grad = cur[part(piece), :] + rs_final(BWD_ATTN, layer, piece)
+            cur[part(piece), :] = grad
+
+            @pl.when(step < layers - 1)
+            def _():
+                begin_back(layer - 1, piece, grad)
+
         if inside:
 
             @pl.when(step == layers - 1)
@@ -740,7 +760,7 @@
         return carry
 
     lax.fori_loop(0, layers, backward, 0)
-    store = pltpu.make_async_copy(cur, tgrad_hbm, w_sem.at[7])
+    store = pltpu.make_async_copy(cur, tgrad_hbm, w_sem.at[8])
     store.start()
     if inside:
         older = [
@@ -871,8 +891,8 @@
         last = [
             pltpu.VMEM((2, rows_each, hidden), F32),
             dma((2,)),
-            pltpu.VMEM((4, layers, 8, wide), F32),
-            pltpu.VMEM((2 + FAR_SIDE, layers, 8, wide), F32),
+            pltpu.VMEM((4, layers, 8, wide), BF16),
+            pltpu.VMEM((2 + FAR_SIDE, layers, 8, wide), BF16),
             pltpu.VMEM((layers, FAR_SIDE, rows_each, total_width), BF16),
             pltpu.VMEM((layers, FAR_SIDE - 1, rows_each, total_width), BF16),
             dma((layers, 4, FAR_SIDE)),
@@ -920,7 +940,7 @@
             pltpu.VMEM((shard, width), F32),
         ]
         + [pltpu.VMEM((CHUNKS, chunk, width), BF16)] * 6
-        + [pltpu.VMEM((CHUNKS, chunk, width), F32), pltpu.SemaphoreType.DMA((8,))]
+        + [pltpu.VMEM((CHUNKS, chunk, width), F32), pltpu.SemaphoreType.DMA((9,))]
         + [sems] * 12
         + last
         + [pltpu.VMEM((layers, 8, wide), F32)],

time: 222 us -> 215 us (0.968)
  Pallas kernels: 221 us -> 213 us
    pallas_call x1, Pallas kernels: 217 us -> 209 us  [body(): pl.pallas_call(partial(step_kernel, inside), name='encoder_step', out_sha...]
where the time goes in v5:
time: 215 us; the launch traced here: 214 us
  Pallas kernels  213 us (99%)
    pallas_call x1, Pallas kernels, body(): pl.pallas_call(partial(step_kernel, inside), name='encoder_step', out_sha...  209 us

profile of v5, /device:TPU:0, one launch (start us, length us, event | category | flops | bytes accessed | tf_op | source)
XLA Modules:
  0.0 213.8 jit_solution(9444451955620606539)
XLA Ops:
  0.6 208.9 %encoder_step.1 = (f32[256,768]{1,0:T(8,128)}, f32[256,768]{1,0:T(8,128)}, f32[2,8,768]{2,1,0:T(8,128)}, f32[2,96,2432]{2,1,0:T(8,128)}) custom-call(bf16[256,768]{1,0:T(8,128)(2,1)} %refs_0_.1, bf16[256,768]{1,0:T(8,128)(2,1)} %refs_1_.1, bf16[2,4,768]{2,1,0:T(4,128)(2,1)} %refs_2_.1, bf16[2,2,768]{2,1,0:T(2,128)(2,1)} %refs_3_.1, bf16[2,768]{1,0:T(2,128)(2,1)} %refs_4_.1, ...), custom_call_target="tpu_custom_call" | custom-call | tf_op jit(solution)/shard_map/encoder_step/pallas_call | solution.py:907
  209.6 4.0 %finish.1 = (f32[256,768]{1,0:T(8,128)}, f32[256,768]{1,0:T(8,128)}, f32[2,3,96,192]{3,2,1,0:T(8,128)}, f32[2,2,24]{2,1,0:T(2,128)}, f32[2,192,96]{2,1,0:T(8,128...) custom-call(f32[256,768]{1,0:T(8,128)} %get-tuple-element.24.result,, ...), custom_call_target="tpu_custom_call" | custom-call | tf_op jit(solution)/shard_map/finish/pallas_call | solution.py:834

commit v6 on v5

--- a/solution.py
+++ b/solution.py
@@ -740,7 +740,6 @@
             @pl.when(step < layers - 1)
             def _():
                 near_add(layer, UP)
-                near_add(layer, OUT)
 
         for piece in range(CHUNKS):
             grad = cur[part(piece), :] + rs_final(BWD_ATTN, layer, piece)
@@ -749,6 +748,8 @@
             @pl.when(step < layers - 1)
             def _():
                 begin_back(layer - 1, piece, grad)
+                if piece == 0:
+                    near_add(layer, OUT)
 
         if inside:
 

time: 215 us -> 212 us (0.986)
  no operation moved by 1% of the time
where the time goes in v6:
time: 212 us
  Pallas kernels  211 us (100%)
    pallas_call x1, Pallas kernels, body(): pl.pallas_call(partial(step_kernel, inside), name='encoder_step', out_sha...  207 us

profile of v6, /device:TPU:0, one launch (start us, length us, event | category | flops | bytes accessed | tf_op | source)
XLA Modules:
  0.0 212.2 jit_solution(16883640623785841897)
XLA Ops:
  0.6 207.4 %encoder_step.1 = (f32[256,768]{1,0:T(8,128)}, f32[256,768]{1,0:T(8,128)}, f32[2,8,768]{2,1,0:T(8,128)}, f32[2,96,2432]{2,1,0:T(8,128)}) custom-call(bf16[256,768]{1,0:T(8,128)(2,1)} %refs_0_.1, bf16[256,768]{1,0:T(8,128)(2,1)} %refs_1_.1, bf16[2,4,768]{2,1,0:T(4,128)(2,1)} %refs_2_.1, bf16[2,2,768]{2,1,0:T(2,128)(2,1)} %refs_3_.1, bf16[2,768]{1,0:T(2,128)(2,1)} %refs_4_.1, ...), custom_call_target="tpu_custom_call" | custom-call | tf_op jit(solution)/shard_map/encoder_step/pallas_call | solution.py:908
  208.0 4.0 %finish.1 = (f32[256,768]{1,0:T(8,128)}, f32[256,768]{1,0:T(8,128)}, f32[2,3,96,192]{3,2,1,0:T(8,128)}, f32[2,2,24]{2,1,0:T(2,128)}, f32[2,192,96]{2,1,0:T(8,128...) custom-call(f32[256,768]{1,0:T(8,128)} %get-tuple-element.24.result,, ...), custom_call_target="tpu_custom_call" | custom-call | tf_op jit(solution)/shard_map/finish/pallas_call | solution.py:835
